TPU v7x, 32 devices: a whole 2x2x4 slice. The times are simulated.
32 devices in a mesh: axial: 16 (over z, y, core), trans: 2 (over x).
Axes of the slice: x: 2, y: 2, z: 4, core: 2. Of those that a mesh axis runs over, the one named last changes fastest.
Arguments:
- source: float32 [128, 512, 512], P('axial', 'trans'), may hold values from -6 to 6
- labels: int32 [128, 512, 512], P('axial', 'trans'), may hold values from 0 to 3
- voltages: float32 [4], replicated, may hold values from -2 to 2
- relax: float32 [2, 512], replicated, may hold values from 0.3 to 1
Outputs:
- potential: float32 [128, 512, 512], P('axial', 'trans')
All inputs are finite; a program needn't handle non-finite values.
Results may differ from a plain program's by a relative error of at most 0.00008.
Values sent between devices are 32-bit elements; how exact they have to be, the bound alone decides.
No kernel may reach another device: no remote copies, remote signals or barrier semaphores. Data moves between devices by JAX's collectives and lax.ppermute only.
A program may use at most 128 MiB of HBM per device.

v0:
```python
import jax
import jax.numpy as jnp
from jax import lax
from jax.sharding import PartitionSpec as P

NX = 512
NY = 512


def from_partner(block, axis, bit):
    count = lax.axis_size(axis)
    route = []
    for low in range(count):
        high = low | 1 << bit
        if high != low and high < count:
            route += [(low, high), (high, low)]
    return lax.ppermute(block, axis, route)


def padded_2(shard, sides, width):
    for axis, dim in sides:
        count, length = (lax.axis_size(axis), shard.shape[dim])
        up = [(i, (i + 1) % count) for i in range(count - 1)]
        down = [(j, i) for i, j in up]
        last = lax.slice_in_dim(shard, length - width, length, axis=dim)
        initial = lax.slice_in_dim(shard, 0, width, axis=dim)
        before = lax.ppermute(last, axis, up)
        after = lax.ppermute(initial, axis, down)
        shard = jnp.concatenate([before, shard, after], axis=dim)
    return shard


def sine_table(count):
    index = jnp.arange(count, dtype=jnp.float32)
    scale = jnp.sqrt(2.0 / (count + 1.0))
    basis = scale * jnp.sin(
        jnp.pi * (index[:, None] + 1.0) * (index[None, :] + 1.0) / (count + 1.0)
    )
    eigen = 2.0 - 2.0 * jnp.cos(jnp.pi * (index + 1.0) / (count + 1.0))
    return (basis, eigen)


def mirror_in(slab):
    ax_count = lax.axis_size("axial")
    digits = ax_count.bit_length() - 1
    for bit in range(digits):
        slab = from_partner(slab, "axial", bit)
    return slab


def mirror_out(slab):
    ax_count = lax.axis_size("axial")
    digits = ax_count.bit_length() - 1
    for bit in range(digits):
        slab = from_partner(slab, "axial", bit)
    return slab


def on_device(source, labels, voltages, relax):
    high = lax.Precision.HIGHEST
    rows = source.shape[1]
    ax_count = lax.axis_size("axial")
    position = lax.axis_index("axial")
    lower = position < ax_count // 2
    basis_x, eigen_x = sine_table(NX)
    basis_y, eigen_y = sine_table(NY)
    row_start = lax.axis_index("trans") * rows
    columns = lax.dynamic_slice_in_dim(basis_x, row_start, rows, 1)
    charge = source
    for region in range(voltages.shape[0]):
        charge = charge + jnp.where(labels == region, voltages[region], 0.0)
    mirrored = mirror_in(charge)[::-1]
    folded = jnp.where(lower, 0.5 * (charge + mirrored), 0.5 * (charge - mirrored))
    inner = jnp.einsum("zxy,jy->zxj", folded, basis_y, precision=high)
    modes = lax.psum(jnp.einsum("kx,zxj->kzj", columns, inner, precision=high), "trans")
    weight_even = relax[0]
    weight_odd = relax[1]
    weight = jnp.where(lower, weight_even, weight_odd)[:, None, None]
    diag = eigen_x[:, None, None] + eigen_y[None, None, :] + 2.0
    first = weight * modes / diag
    padded = padded_2(first, (("axial", 1),), 1)
    below = padded[:, :-2]
    above = padded[:, 2:]
    second = first + weight * (modes - diag * first + below + above) / diag
    back = jnp.einsum("kzj,jy->kzy", second, basis_y, precision=high)
    field = jnp.einsum("kx,kzy->zxy", columns, back, precision=high)
    partner = mirror_out(field)[::-1]
    return field + jnp.where(lower, -1.0, 1.0) * partner


def solution(mesh):
    placed = (P("axial", "trans", None), P("axial", "trans", None), P(), P())
    return jax.shard_map(
        on_device, mesh=mesh, in_specs=placed, out_specs=P("axial", "trans", None), check_vma=False
    )
```

profile of v0, /device:TPU:9, one launch (start us, length us, event | category | flops | bytes accessed | tf_op | source)
XLA Modules:
  0.0 1097.0 jit_solution(4861309574738589126)
XLA Ops:
  6.5 0.0 all-reduce.2.cloned.1.call-start
  6.5 1.5 fusion.42
  8.0 6.9 select_add_fusion
  14.9 0.0 copy-start
  14.9 2.0 copy-done
  16.9 0.7 collective-permute-start
  17.6 6.8 collective-permute-done
  24.4 1.2 collective-permute-start.1
  25.6 90.5 %collective-permute-done.1 = f32[8,256,512]{2,1,0:T(8,128)S(1)} collective-permute-done((f32[8,256,512]{2,1,0:T(8,128)S(1)}, f32[8,256,512]{2,1,0:T(8,128)S(1)}, u32[]{:S(2)}, u32[]{:S(2)}) %collective-permute-start.1) | collective-permute-done | bytes 4194336 | tf_op jit(solution)/shard_map/ppermute | solution.py:17
  116.2 0.3 collective-permute-start.2
  116.4 90.7 %collective-permute-done.2 = f32[8,256,512]{2,1,0:T(8,128)} collective-permute-done((f32[8,256,512]{2,1,0:T(8,128)S(1)}, f32[8,256,512]{2,1,0:T(8,128)}, u32[]{:S(2)}, u32[]{:S(2)}) %collective-permute-start.2) | collective-permute-done | bytes 4194336 | tf_op jit(solution)/shard_map/ppermute | solution.py:17
  207.1 2.3 collective-permute-start.3
  209.4 3.6 sine_multiply_fusion
  213.0 176.8 %collective-permute-done.3 = f32[8,256,512]{2,1,0:T(8,128)} collective-permute-done((f32[8,256,512]{2,1,0:T(8,128)}, f32[8,256,512]{2,1,0:T(8,128)}, u32[]{:S(2)}, u32[]{:S(2)}) %collective-permute-start.3) | collective-permute-done | bytes 4194336 | tf_op jit(solution)/shard_map/ppermute | solution.py:17
  389.8 4.6 rev.6
  394.4 14.6 %fusion.8 = f32[8,256,512]{2,1,0:T(8,128)S(1)} fusion(f32[8,256,512]{2,1,0:T(8,128)} %copy-done, f32[8,256,512]{2,1,0:T(8,128)} %rev.6, pred[]{:T(512)S(6)} %lt.6, f32[512]{0:T(512)S(1)} %get-tuple-element.11, f32[512]{0:T(512)S(1)} %get-tuple-element.12), kind=kOutput, calls=%fused_computation.11 | convolution fusion | flops 6448480256 | bytes 12587009 | tf_op jit(solution)/shard_map/zxy,jy->zxj/dot_general | solution.py:74
  409.0 9.1 fusion.20
  418.1 0.0 copy-start.3
  418.1 0.0 all-reduce.2.cloned.1.call-update
  418.2 0.6 copy-done.3
  418.8 0.1 add_add_fusion
  418.9 199.1 %all-reduce.2.cloned.1.call-done = f32[512,8,512]{2,0,1:T(8,128)} async-done(((f32[512,8,512]{2,0,1:T(8,128)}), f32[512,8,512]{2,0,1:T(8,128)}) %all-reduce.2.cloned.1.call-update) | async-done | bytes 8388624 | tf_op jit(solution)/shard_map/psum | solution.py:75
  618.1 4.9 multiply_divide_fusion
  623.0 0.0 copy-start.2
  623.0 3.2 copy-done.2
  626.2 0.2 fusion.41
  626.4 3.7 collective-permute-start.4
  630.1 1.9 collective-permute-start.5
  632.0 21.0 %collective-permute-done.4 = f32[512,1,512]{2,0,1:T(8,128)S(1)} collective-permute-done((f32[512,1,512]{2,0,1:T(8,128)S(1)}, f32[512,1,512]{2,0,1:T(8,128)S(1)}, u32[]{:S(2)}, u32[]{:S(2)}) %collective-permute-start.4) | collective-permute-done | bytes 1048608 | tf_op jit(solution)/shard_map/ppermute | solution.py:27
  653.0 1.6 collective-permute-done.5
  654.6 40.0 %fusion.5 = f32[512,8,512]{0,2,1:T(8,128)} fusion(f32[512,8,512]{2,0,1:T(8,128)} %copy-done.2, f32[512,1,512]{2,0,1:T(8,128)S(1)} %collective-permute-done.5, f32[512,1,512]{2,0,1:T(8,128)S(1)} %collective-permute-done.4, f32[512,8,512]{2,0,1:T(8,128)} %all-reduce.2.cloned.1.call-done, f32[512,512]{1,0:T(8,128)S(1)} %add_add_fusion, f32[512]{0:T(512)S(1)} %bitcast.20, ...), kind=kOutput, calls=%fused_computation.8 | convolution fusion | flops 12904562688 | bytes 28317696 | tf_op jit(solution)/shard_map/kzj,jy->kzy/dot_general | solution.py:85
  694.6 9.1 convolution_bitcast_fusion
  703.8 0.0 copy-start.1
  703.8 2.0 copy-done.1
  705.8 0.0 collective-permute-start.6
  705.8 7.2 collective-permute-done.6
  712.9 0.6 collective-permute-start.7
  713.6 91.4 %collective-permute-done.7 = f32[8,256,512]{1,2,0:T(8,128)S(1)} collective-permute-done((f32[8,256,512]{1,2,0:T(8,128)S(1)}, f32[8,256,512]{1,2,0:T(8,128)S(1)}, u32[]{:S(2)}, u32[]{:S(2)}) %collective-permute-start.7) | collective-permute-done | bytes 4194336 | tf_op jit(solution)/shard_map/ppermute | solution.py:17
  805.0 0.0 collective-permute-start.8
  805.0 91.2 %collective-permute-done.8 = f32[8,256,512]{1,2,0:T(8,128)} collective-permute-done((f32[8,256,512]{1,2,0:T(8,128)S(1)}, f32[8,256,512]{1,2,0:T(8,128)}, u32[]{:S(2)}, u32[]{:S(2)}) %collective-permute-start.8) | collective-permute-done | bytes 4194336 | tf_op jit(solution)/shard_map/ppermute | solution.py:17
  896.2 2.1 collective-permute-start.9
  898.3 180.5 %collective-permute-done.9 = f32[8,256,512]{1,2,0:T(8,128)} collective-permute-done((f32[8,256,512]{1,2,0:T(8,128)}, f32[8,256,512]{1,2,0:T(8,128)}, u32[]{:S(2)}, u32[]{:S(2)}) %collective-permute-start.9) | collective-permute-done | bytes 4194336 | tf_op jit(solution)/shard_map/ppermute | solution.py:17
  1078.8 6.0 multiply_add_fusion
  1084.8 5.3 copy.5
  (3 shorter events, 0.1 us)
Async XLA Ops:
  6.5 611.5 %all-reduce.2.cloned.1.call-start = ((), (), s32[]{:S(2)}) async-start(), calls=%async_computation | async-start | bytes 16777216 | tf_op jit(solution)/shard_map/psum | solution.py:75
  14.9 2.0 copy-start
  16.9 7.5 collective-permute-start
  24.4 91.8 %collective-permute-start.1 = (f32[8,256,512]{2,1,0:T(8,128)S(1)}, f32[8,256,512]{2,1,0:T(8,128)S(1)}, u32[]{:S(2)}, u32[]{:S(2)}) collective-permute-start(f32[8,256,512]{2,1,0:T(8,128)S(1)} %collective-permute-done), channel_id=1, source_target_pairs={{0,4},{4,0},{2,6},{6,2},{8,12},{12,8},{10,14},{14,10},{16,20},{20,... | collective-permute-start | bytes 12582920 | tf_op jit(solution)/shard_map/ppermute | solution.py:17
  116.2 91.0 %collective-permute-start.2 = (f32[8,256,512]{2,1,0:T(8,128)S(1)}, f32[8,256,512]{2,1,0:T(8,128)}, u32[]{:S(2)}, u32[]{:S(2)}) collective-permute-start(f32[8,256,512]{2,1,0:T(8,128)S(1)} %collective-permute-done.1), channel_id=1, source_target_pairs={{0,8},{8,0},{2,10},{10,2},{4,12},{12,4},{6,14},{14,6},{16,24},{24,... | collective-permute-start | bytes 12582920 | tf_op jit(solution)/shard_map/ppermute | solution.py:17
  207.1 182.7 %collective-permute-start.3 = (f32[8,256,512]{2,1,0:T(8,128)}, f32[8,256,512]{2,1,0:T(8,128)}, u32[]{:S(2)}, u32[]{:S(2)}) collective-permute-start(f32[8,256,512]{2,1,0:T(8,128)} %collective-permute-done.2), channel_id=1, source_target_pairs={{0,16},{16,0},{2,18},{18,2},{4,20},{20,4},{6,22},{22,6},{8,24},{24... | collective-permute-start | bytes 12582920 | tf_op jit(solution)/shard_map/ppermute | solution.py:17
  418.1 0.7 copy-start.3
  623.0 3.2 copy-start.2
  626.4 26.6 %collective-permute-start.4 = (f32[512,1,512]{2,0,1:T(8,128)S(1)}, f32[512,1,512]{2,0,1:T(8,128)S(1)}, u32[]{:S(2)}, u32[]{:S(2)}) collective-permute-start(f32[512,1,512]{2,0,1:T(8,128)S(1)} %get-tuple-element.5), channel_id=1, source_target_pairs={{0,2},{2,4},{4,6},{6,8},{8,10},{10,12},{12,14},{14,16},{16,18},{18... | collective-permute-start | bytes 3145736 | tf_op jit(solution)/shard_map/ppermute | solution.py:27
  630.1 24.6 %collective-permute-start.5 = (f32[512,1,512]{2,0,1:T(8,128)S(1)}, f32[512,1,512]{2,0,1:T(8,128)S(1)}, u32[]{:S(2)}, u32[]{:S(2)}) collective-permute-start(f32[512,1,512]{2,0,1:T(8,128)S(1)} %get-tuple-element.6), channel_id=1, source_target_pairs={{2,0},{4,2},{6,4},{8,6},{10,8},{12,10},{14,12},{16,14},{18,16},{20... | collective-permute-start | bytes 3145736 | tf_op jit(solution)/shard_map/ppermute | solution.py:28
  703.8 2.0 copy-start.1
  705.8 7.2 collective-permute-start.6
  712.9 92.0 %collective-permute-start.7 = (f32[8,256,512]{1,2,0:T(8,128)S(1)}, f32[8,256,512]{1,2,0:T(8,128)S(1)}, u32[]{:S(2)}, u32[]{:S(2)}) collective-permute-start(f32[8,256,512]{1,2,0:T(8,128)S(1)} %collective-permute-done.6), channel_id=1, source_target_pairs={{0,4},{4,0},{2,6},{6,2},{8,12},{12,8},{10,14},{14,10},{16,20},{20,... | collective-permute-start | bytes 12582920 | tf_op jit(solution)/shard_map/ppermute | solution.py:17
  805.0 91.2 %collective-permute-start.8 = (f32[8,256,512]{1,2,0:T(8,128)S(1)}, f32[8,256,512]{1,2,0:T(8,128)}, u32[]{:S(2)}, u32[]{:S(2)}) collective-permute-start(f32[8,256,512]{1,2,0:T(8,128)S(1)} %collective-permute-done.7), channel_id=1, source_target_pairs={{0,8},{8,0},{2,10},{10,2},{4,12},{12,4},{6,14},{14,6},{16,24},{24,... | collective-permute-start | bytes 12582920 | tf_op jit(solution)/shard_map/ppermute | solution.py:17
  896.2 182.6 %collective-permute-start.9 = (f32[8,256,512]{1,2,0:T(8,128)}, f32[8,256,512]{1,2,0:T(8,128)}, u32[]{:S(2)}, u32[]{:S(2)}) collective-permute-start(f32[8,256,512]{1,2,0:T(8,128)} %collective-permute-done.8), channel_id=1, source_target_pairs={{0,16},{16,0},{2,18},{18,2},{4,20},{20,4},{6,22},{22,6},{8,24},{24... | collective-permute-start | bytes 12582920 | tf_op jit(solution)/shard_map/ppermute | solution.py:17
Sparse Core Ops, SparseCore 0:
  418.2 199.7 all-reduce.1
where the time goes:
time: 1100 us
  waiting for transfers between devices  957 us (87%)
  matrix products  72.8 us (7%)
  other arithmetic  21.5 us (2%)
  local copies, waits for them, and re-layouts  19.4 us (2%)
  between operations  13.5 us (1%)
  starting transfers between devices  12.8 us (1%)
    ppermute x8, waiting for transfers between devices, from_partner(): return lax.ppermute(block, axis, route)  735 us
    psum x1, waiting for transfers between devices, on_device(): lax.psum(jnp.einsum('kx,zxj->kzj', columns, inner, precision=high), 'trans')  199 us
    dot_general x1, matrix products, on_device(): back = jnp.einsum('kzj,jy->kzy', second, basis_y, precision=high)  40 us
  transfers between devices with their start and end apart: 11, of which 11 were waited for; matrix products, arithmetic and copies ran while one was open for 0% of the time, Pallas kernels for 0%

commit v1 on v0

v1 whole, which is shorter than its diff:
```python
import jax
import jax.numpy as jnp
import ml_dtypes
import numpy as np
from jax import lax
from jax.experimental import pallas as pl
from jax.experimental.pallas import tpu as pltpu
from jax.sharding import PartitionSpec as P

NX = 512
NY = 512
F32 = jnp.float32
BF16 = jnp.bfloat16
VMEM_LIMIT = 48 * 1024 * 1024


def table_parts():
    f = np.float32
    index = np.arange(NX, dtype=f) + f(1)
    inverse = f(1) / f(NX + 1)
    angle = ((f(np.pi) * index[:, None]) * index[None, :]) * inverse
    basis = np.sqrt(f(2) / f(NX + 1)).astype(f) * np.sin(angle.astype(np.float64)).astype(f)
    high = basis.astype(ml_dtypes.bfloat16)
    low = (basis - high.astype(f)).astype(ml_dtypes.bfloat16)
    return high, low


BASIS = table_parts()
BASIS_T = tuple(np.ascontiguousarray(part.T) for part in BASIS)


def split(x):
    high = x.astype(BF16)
    return high, (x - high.astype(F32)).astype(BF16)


def dot3(left, right):
    def dot(a, b):
        return jnp.dot(a, b, preferred_element_type=F32)

    return dot(left[0], right[0]) + (dot(left[0], right[1]) + dot(left[1], right[0]))


def after(value, *others):
    return lax.optimization_barrier((value,) + others)[0]


def whole(shape):
    return pl.BlockSpec(shape, lambda g: (0,) * len(shape))


def call(body, grid, in_specs, out_specs, out_shape, flops, size, scratch=(), aliases=None):
    return pl.pallas_call(
        body,
        grid=(grid,),
        in_specs=in_specs,
        out_specs=out_specs,
        out_shape=out_shape,
        scratch_shapes=scratch,
        input_output_aliases=aliases or {},
        compiler_params=pltpu.CompilerParams(
            dimension_semantics=("arbitrary",), vmem_limit_bytes=VMEM_LIMIT
        ),
        cost_estimate=pl.CostEstimate(flops=flops, bytes_accessed=size, transcendentals=0),
    )


def rows_body(volts, source, labels, high, low, out):
    label = labels[...]
    pick = jnp.full(label.shape, volts[0], F32)
    for region in range(1, volts.shape[0]):
        pick = jnp.where(label == region, volts[region], pick)
    out[...] = dot3(split(source[...] + pick), (high[...], low[...]))


def row_modes(source, labels, voltages, chunk):
    rows = source.shape[1]
    count, start, step = chunk
    plane = pl.BlockSpec((None, rows, NY), lambda g: (start + step * g, 0, 0))
    return call(
        rows_body,
        count,
        [pl.BlockSpec(memory_space=pltpu.SMEM), plane, plane, whole((NY, NY)), whole((NY, NY))],
        pl.BlockSpec((None, rows, NY), lambda g: (g, 0, 0)),
        jax.ShapeDtypeStruct((count, rows, NY), F32),
        6 * count * rows * NY * NY,
        12 * count * rows * NY,
    )(voltages, source, labels, jnp.asarray(BASIS_T[0]), jnp.asarray(BASIS_T[1]))


def modes_body(parts, aliased):
    def body(*refs):
        high, low = refs[:2]
        rows = [ref[...] for ref in refs[2:2 + parts]]
        out = refs[2 + parts + aliased]
        out[...] = dot3((high[...], low[...]), split(jnp.concatenate(rows, axis=0)))

    return body


def x_modes(table, parts, total, chunk, buffer):
    rows = parts[0].shape[1]
    count, start, step = chunk
    plane = pl.BlockSpec((None, rows, NY), lambda g: (g, 0, 0))
    aliased = 0 if buffer is None else 1
    return call(
        modes_body(len(parts), aliased),
        count,
        [whole((NX, NX))] * 2 + [plane] * len(parts) + [pl.BlockSpec(memory_space=pl.ANY)] * aliased,
        pl.BlockSpec((None, NX, NY), lambda g: (start + step * g, 0, 0)),
        jax.ShapeDtypeStruct((total, NX, NY), F32),
        6 * count * NX * NX * NY,
        8 * count * NX * NY,
        aliases={2 + len(parts): 0} if aliased else None,
    )(*table, *parts, *([buffer] if aliased else []))


def stencil(inverse, weights, own, other, last_plane, plane, extra):
    keep_low = jnp.where(plane > 0, 1.0, 0.0)
    keep_high = jnp.where(plane < last_plane, 1.0, 0.0)
    edge = 1.0 - keep_low * keep_high
    inv = inverse[...]
    near = weights[:, 0:1] * own[1][...] + weights[:, 1:2] * other[1][...]
    far = weights[:, 2:3] * (keep_low * own[0][...] + keep_high * own[2][...])
    far = far + weights[:, 3:4] * (keep_low * other[0][...] + keep_high * other[2][...])
    return inv * (near + inv * far) + edge * extra[...]


def back_to_grid(total, rows_table, table):
    return dot3(split(dot3(rows_table, split(total))), table)


def halves(refs):
    return tuple(ref[...] for ref in refs)


def plane_specs(place, last_plane):
    def at(shift):
        def index(g):
            return (jnp.clip(place(g) + shift, 0, last_plane), 0, 0)

        return pl.BlockSpec((None, NX, NY), index)

    return [at(-1), at(0), at(1)]


def extra_spec(place, middle):
    return pl.BlockSpec((None, NX, NY), lambda g: (jnp.where(place(g) < middle, 0, 1), 0, 0))


def finished_planes(count, place, inverse, weights, own, other, extra, rows_table, table, buffer):
    total, rows = own.shape[0], rows_table[0].shape[0]
    aliased = 0 if buffer is None else 1

    def body(*refs):
        inv, wts = refs[:2]
        out = refs[-1]
        modes = stencil(inv, wts, refs[2:5], refs[5:8], total - 1, place(pl.program_id(0)), refs[8])
        out[...] = back_to_grid(modes, halves(refs[9:11]), halves(refs[11:13]))

    return call(
        body,
        count,
        [whole((NX, NY)), whole((NX, 128))]
        + plane_specs(place, total - 1) * 2
        + [extra_spec(place, total // 2)]
        + [whole((rows, NX))] * 2 + [whole((NY, NY))] * 2
        + [pl.BlockSpec(memory_space=pl.ANY)] * aliased,
        pl.BlockSpec((None, rows, NY), lambda g: (place(g), 0, 0)),
        jax.ShapeDtypeStruct((total, rows, NY), F32),
        count * (6 * rows * NX * NY + 6 * rows * NY * NY),
        count * 28 * NX * NY,
        aliases={13: 0} if aliased else None,
    )(inverse, weights, *[own] * 3, *[other] * 3, extra, *rows_table, *table, *([buffer] if aliased else []))


def base_planes(start, missing, inverse, weights, own, other, extra):
    total = own.shape[0]

    def place(g):
        return start + g

    def body(*refs):
        plane = place(pl.program_id(0))
        others = [jnp.where(plane + shift == missing, 0.0, ref[...]) for shift, ref in zip((-1, 0, 1), refs[5:8])]
        refs[-1][...] = stencil(refs[0], refs[1], refs[2:5], others, total - 1, plane, refs[8])

    return call(
        body,
        3,
        [whole((NX, NY)), whole((NX, 128))] + plane_specs(place, total - 1) * 2 + [extra_spec(place, total // 2)],
        pl.BlockSpec((None, NX, NY), lambda g: (g, 0, 0)),
        jax.ShapeDtypeStruct((3, NX, NY), F32),
        3 * 12 * NX * NY,
        3 * 32 * NX * NY,
    )(inverse, weights, *[own] * 3, *[other] * 3, extra)


def last_planes(start, inverse, weights, base, x_table, parts, rows_table, table, buffer):
    total, rows = buffer.shape[0], buffer.shape[1]
    count = len(parts)

    def body(*refs):
        inv, wts, base_ref = refs[:3]
        pieces = refs[5:5 + count]
        near_rows, grid_table = refs[5 + count:7 + count], refs[7 + count:9 + count]
        out, late = refs[-2:]
        step = pl.program_id(0)

        @pl.when(step == 0)
        def _():
            rows_in = jnp.concatenate([ref[...] for ref in pieces], axis=0)
            late[...] = dot3(halves(refs[3:5]), split(rows_in))

        scale = jnp.where(step == 1, 1.0, 0.0)
        factor = scale * wts[:, 1:2] + (1.0 - scale) * inv[...] * wts[:, 3:4]
        modes = base_ref[...] + inv[...] * (factor * late[...])
        out[...] = back_to_grid(modes, halves(near_rows), halves(grid_table))

    length = parts[0].shape[1]
    width = x_table[0].shape[1]
    return call(
        body,
        3,
        [whole((NX, NY)), whole((NX, 128)), pl.BlockSpec((None, NX, NY), lambda g: (g, 0, 0))]
        + [whole((NX, width))] * 2
        + [pl.BlockSpec((None, length, NY), lambda g: (0, 0, 0))] * count
        + [whole((rows, NX))] * 2 + [whole((NY, NY))] * 2 + [pl.BlockSpec(memory_space=pl.ANY)],
        pl.BlockSpec((None, rows, NY), lambda g: (start + g, 0, 0)),
        jax.ShapeDtypeStruct((total, rows, NY), F32),
        6 * NX * width * NY + 3 * (6 * rows * NX * NY + 6 * rows * NY * NY),
        3 * 8 * NX * NY,
        scratch=[pltpu.VMEM((NX, NY), F32)],
        aliases={9 + count: 0},
    )(inverse, weights, base, *x_table, *parts, *rows_table, *table, buffer)


def to_mirror(block):
    count = lax.axis_size("axial")
    return lax.ppermute(block, "axial", [(i, count - 1 - i) for i in range(count)])


def gather_rows(block):
    count = lax.axis_size("trans")
    parts = [block]
    for step in range(1, count):
        route = [(i, (i - step) % count) for i in range(count)]
        parts.append(lax.ppermute(block, "trans", route))
    return parts


def halo(first, last):
    count = lax.axis_size("axial")
    up = [(i, i + 1) for i in range(count - 1) if i + 1 != count // 2]
    below = lax.ppermute(last, "axial", up)
    above = lax.ppermute(first, "axial", [(j, i) for i, j in up])
    return below, above


def on_device(source, labels, voltages, relax):
    planes, rows = source.shape[0], source.shape[1]
    half = planes // 2
    ax_count = lax.axis_size("axial")
    position = lax.axis_index("axial")
    row_start = lax.axis_index("trans") * rows

    chunk_a = (2, 0, planes - 1)
    chunk_b = (half - 2, 1, 1)
    chunk_c = (half - 2, half + 1, 1)
    chunk_d = (1, half - 1, 1)
    chunk_e = (1, half, 1)
    chunks = [chunk_a, chunk_b, chunk_c, chunk_d, chunk_e]

    def mirrored(chunk):
        return chunk[0], planes - 1 - chunk[1], -chunk[2]

    inner = [row_modes(source, labels, voltages, chunk) for chunk in chunks]

    x_table = tuple(
        lax.dynamic_slice_in_dim(jnp.concatenate([part, part], axis=1), row_start, NX, 1)
        for part in (jnp.asarray(BASIS[0]), jnp.asarray(BASIS[1]))
    )
    rows_table = tuple(
        lax.dynamic_slice_in_dim(jnp.asarray(part), row_start, rows, 0) for part in BASIS_T
    )
    table = tuple(jnp.asarray(part) for part in BASIS)

    index = jnp.arange(NX, dtype=F32) + 1.0
    eigen = 2.0 - 2.0 * jnp.cos(jnp.pi * index / (NX + 1.0))
    inverse = 1.0 / (eigen[:, None] + eigen[None, :] + 2.0)
    even, odd = relax[0], relax[1]
    a_even, a_odd = (2.0 - even) * even, (2.0 - odd) * odd
    b_even, b_odd = even * even, odd * odd
    columns = [0.5 * (a_even + a_odd), 0.5 * (a_even - a_odd), 0.5 * (b_even + b_odd), 0.5 * (b_even - b_odd)]
    weights = jnp.pad(jnp.stack(columns, axis=1), ((0, 0), (0, 124)))
    beta, beta_cross = columns[2][:, None], columns[3][:, None]
    cross = (even * odd)[:, None] * inverse * inverse

    m_a, o_a = to_mirror(inner[0]), gather_rows(inner[0])
    m_b, o_b = to_mirror(inner[1]), gather_rows(inner[1])
    own = x_modes(x_table, o_a, planes, chunk_a, None)
    below, above = halo(own[0], own[planes - 1])
    m_c = to_mirror(after(inner[2], m_a))
    x_a = gather_rows(m_a)
    o_c = gather_rows(after(inner[2], own))
    own = x_modes(x_table, o_b, planes, chunk_b, own)
    other = x_modes(x_table, x_a, planes, mirrored(chunk_a), None)
    below_2, above_2 = halo(other[0], other[planes - 1])
    m_d = to_mirror(after(inner[3], m_b))
    x_b = gather_rows(m_b)
    o_d = gather_rows(after(inner[3], own))
    own = x_modes(x_table, o_c, planes, chunk_c, own)
    o_e = gather_rows(after(inner[4], own))
    other = x_modes(x_table, x_b, planes, mirrored(chunk_b), other)
    own = x_modes(x_table, o_d, planes, chunk_d, own)
    m_e = to_mirror(after(inner[4], m_c))
    x_c = gather_rows(m_c)
    own = x_modes(x_table, o_e, planes, chunk_e, own)
    at_bottom = jnp.where(position == ax_count // 2, 1.0, 0.0)
    at_top = jnp.where(position == ax_count // 2 - 1, 1.0, 0.0)
    extra = jnp.stack([
        inverse * inverse * (beta * below + beta_cross * below_2) + at_bottom * cross * own[0],
        inverse * inverse * (beta * above + beta_cross * above_2) - at_top * cross * own[planes - 1],
    ])
    other = x_modes(x_table, x_c, planes, mirrored(chunk_c), other)

    def outer(g):
        return jnp.where(g < half - 2, g, g + 4)

    out = finished_planes(
        planes - 4, outer, inverse, weights, own, other, extra, rows_table, table, None
    )
    x_d = gather_rows(m_d)
    other = x_modes(x_table, x_d, planes, mirrored(chunk_d), other)
    base = base_planes(half - 2, half - 1, inverse, weights, own, other, extra)
    out = finished_planes(
        1, lambda g: g + half + 1, inverse, weights, own, other, extra, rows_table, table, out
    )
    x_e = gather_rows(m_e)
    return last_planes(half - 2, inverse, weights, base, x_table, x_e, rows_table, table, out)


def solution(mesh):
    placed = (P("axial", "trans", None), P("axial", "trans", None), P(), P())
    return jax.shard_map(
        on_device, mesh=mesh, in_specs=placed, out_specs=P("axial", "trans", None), check_vma=False
    )
```

time: 1100 us -> 278 us (0.25)
  waiting for transfers between devices: 957 us -> 151 us
  Pallas kernels: 0 us -> 79.3 us
  matrix products: 72.8 us -> 0 us
  other arithmetic: 21.5 us -> 3.84 us
  starting transfers between devices: 12.8 us -> 26.8 us
  between operations: 13.5 us -> 0.26 us
    ppermute x10 -> x19, waiting for transfers between devices: 758 us -> 151 us  [the longest x5 119 us: to_mirror(): lax.ppermute(block, 'axial', [(i, count - 1 - i) for i in range(count)])]
    psum x1 -> x0, waiting for transfers between devices: 199 us -> none  [on_device(): lax.psum(jnp.einsum('kx,zxj->kzj', columns, inner, precision=high), 'trans')]
    pallas_call x0 -> x18, Pallas kernels: none -> 79.3 us  [the longest x9 31.9 us: x_modes(): call(modes_body(len(parts), aliased), count, [whole((NX, NX))] * 2 + [pla...]
    dot_general x4 -> x0, matrix products: 72.8 us -> none  [the longest x1 40 us: on_device(): back = jnp.einsum('kzj,jy->kzy', second, basis_y, precision=high)]
    ppermute x10 -> x19, starting transfers between devices: 12.8 us -> 26.8 us  [the longest x5 11.6 us: to_mirror(): lax.ppermute(block, 'axial', [(i, count - 1 - i) for i in range(count)])]
    add x4 -> x0, other arithmetic: 13 us -> none  [the longest x1 6.87 us: on_device(): charge = charge + jnp.where(labels == region, voltages[region], 0.0)]
  transfers between devices with their start and end apart: 11 -> 19, of which waited for: 11 -> 8; matrix products, arithmetic and copies ran while one was open for 0% -> 4% of each run, Pallas kernels for 0% -> 25%
where the time goes in v1:
time: 278 us; the launch traced here: 277 us
  waiting for transfers between devices  151 us (54%)
  Pallas kernels  79.3 us (29%)
  starting transfers between devices  26.8 us (10%)
  local copies, waits for them, and re-layouts  16.5 us (6%)
  other arithmetic  3.84 us (1%)
    ppermute x5, waiting for transfers between devices, to_mirror(): lax.ppermute(block, 'axial', [(i, count - 1 - i) for i in range(count)])  119 us
    pallas_call x9, Pallas kernels, x_modes(): call(modes_body(len(parts), aliased), count, [whole((NX, NX))] * 2 + [pla...  31.9 us
    pallas_call x2, Pallas kernels, finished_planes(): call(body, count, [whole((NX, NY)), whole((NX, 128))] + plane_specs(place...  17.5 us
    ppermute x10, waiting for transfers between devices, gather_rows(): parts.append(lax.ppermute(block, 'trans', route))  16.1 us
    ppermute x2, waiting for transfers between devices, halo(): above = lax.ppermute(first, 'axial', [(j, i) for i, j in up])  15.2 us
    pallas_call x5, Pallas kernels, row_modes(): call(rows_body, count, [pl.BlockSpec(memory_space=pltpu.SMEM), plane, pla...  13.3 us
    ppermute x5, starting transfers between devices, to_mirror(): lax.ppermute(block, 'axial', [(i, count - 1 - i) for i in range(count)])  11.6 us
    pallas_call x1, Pallas kernels, base_planes(): call(body, 3, [whole((NX, NY)), whole((NX, 128))] + plane_specs(place, to...  9.51 us
  transfers between devices with their start and end apart: 19, of which 8 were waited for; matrix products, arithmetic and copies ran while one was open for 4% of the time, Pallas kernels for 25%

profile of v1, /device:TPU:9, one launch (start us, length us, event | category | flops | bytes accessed | tf_op | source)
XLA Modules:
  0.0 277.3 jit_solution(15685089964280893780)
XLA Ops:
  0.0 1.0 copy-done.1
  1.0 1.0 copy-done.3
  2.7 3.3 %shard_map.84.refs_2_ = f32[2,256,512]{2,1,0:T(8,128)} custom-call(f32[4]{0:T(128)S(1)} %copy-done.17, f32[8,256,512]{2,1,0:T(8,128)} %source.9, s32[8,256,512]{2,1,0:T(8,128)} %labels.9, bf16[512,512]{1,0:T(8,128)(2,1)S(1)} %copy-done.1, bf16[512,512]{1,0:T(8,128)(2,1)S(1)} %copy-done.3), custom_call_target="tpu_custom_call" | custom-call | flops 805306368 | bytes 3145728 | tf_op jit(solution)/shard_map/pallas_call | solution.py:80
  6.1 1.2 collective-permute-start
  7.3 3.1 %collective-permute-start.8 = (f32[2,256,512]{2,1,0:T(8,128)}, f32[2,256,512]{2,1,0:T(8,128)}, u32[]{:S(2)}, u32[]{:S(2)}) collective-permute-start(f32[2,256,512]{2,1,0:T(8,128)} %shard_map.84.refs_2_), channel_id=1, source_target_pairs={{0,30},{2,28},{4,26},{6,24},{8,22},{10,20},{12,18},{14,16},{16,14}... | collective-permute-start | bytes 3145736 | tf_op jit(solution)/shard_map/ppermute | solution.py:240
  10.4 3.2 %shard_map.86.refs_2_ = f32[2,256,512]{2,1,0:T(8,128)} custom-call(f32[4]{0:T(128)S(1)} %copy-done.17, f32[8,256,512]{2,1,0:T(8,128)} %source.9, s32[8,256,512]{2,1,0:T(8,128)} %labels.9, bf16[512,512]{1,0:T(8,128)(2,1)S(1)} %copy-done.1, bf16[512,512]{1,0:T(8,128)(2,1)S(1)} %copy-done.3), custom_call_target="tpu_custom_call" | custom-call | flops 805306368 | bytes 3145728 | tf_op jit(solution)/shard_map/pallas_call | solution.py:80
  14.2 2.5 shard_map.83.refs_2_
  16.6 1.3 constant_dynamic-slice_fusion.2
  17.9 12.5 %collective-permute-done.refs_3_ = f32[2,256,512]{2,1,0:T(8,128)} collective-permute-done((f32[2,256,512]{2,1,0:T(8,128)}, f32[2,256,512]{2,1,0:T(8,128)}, u32[]{:S(2)}, u32[]{:S(2)}) %collective-permute-start) | collective-permute-done | bytes 1048608 | tf_op jit(solution)/shard_map/ppermute | solution.py:248
  30.4 4.2 %shard_map.85.refs_4_ = f32[8,512,512]{2,1,0:T(8,128)} custom-call(bf16[512,512]{1,0:T(8,128)(2,1)S(1)} %get-tuple-element.32.refs_0_.refs_3_, bf16[512,512]{1,0:T(8,128)(2,1)S(1)} %get-tuple-element.31.refs_1_.refs_4_, f32[2,256,512]{2,1,0:T(8,128)} %shard_map.84.refs_2_, f32[2,256,512]{2,1,0:T(8,128)} %collective-permute-done.refs_3_), custom_call_target="tpu_custom_call" | custom-call | flops 1610612736 | bytes 4194304 | tf_op jit(solution)/shard_map/pallas_call | solution.py:106
  34.6 1.2 collective-permute-start.1
  35.8 77.6 %collective-permute-done.8.refs_2_ = f32[2,256,512]{2,1,0:T(8,128)} collective-permute-done((f32[2,256,512]{2,1,0:T(8,128)}, f32[2,256,512]{2,1,0:T(8,128)}, u32[]{:S(2)}, u32[]{:S(2)}) %collective-permute-start.8) | collective-permute-done | bytes 1048608 | tf_op jit(solution)/shard_map/ppermute | solution.py:240
  113.6 3.1 %slice_bitcast_fusion.5 = (f32[512,512]{1,0:T(8,128)}, f32[512,512]{1,0:T(8,128)}) fusion(f32[8,512,512]{2,1,0:T(8,128)} %shard_map.85.refs_4_), kind=kLoop, calls=%fused_computation.13 | loop fusion | bytes 4194304 | tf_op jit(solution)/shard_map/squeeze | solution.py:302
  116.7 1.9 collective-permute-start.13
  118.7 2.7 collective-permute-start.9
  121.3 2.2 copy-done
  123.5 1.6 shard_map.89.refs_2_
  125.2 2.6 shard_map.82.refs_2_
  127.8 4.2 %shard_map.87.refs_4_ = f32[8,512,512]{2,1,0:T(8,128)} custom-call(bf16[512,512]{1,0:T(8,128)(2,1)S(1)} %get-tuple-element.32.refs_0_.refs_3_, bf16[512,512]{1,0:T(8,128)(2,1)S(1)} %get-tuple-element.31.refs_1_.refs_4_, f32[2,256,512]{2,1,0:T(8,128)} %shard_map.86.refs_2_, ...), custom_call_target="tpu_custom_call", output_to_operand_aliasing={{}: (4, {})} | custom-call | flops 1610612736 | bytes 4194304 | tf_op jit(solution)/shard_map/pallas_call | solution.py:106
  131.9 17.2 %collective-permute-done.5.refs_2_ = f32[2,256,512]{2,1,0:T(8,128)} collective-permute-done((f32[2,256,512]{2,1,0:T(8,128)}, f32[2,256,512]{2,1,0:T(8,128)}, u32[]{:S(2)}, u32[]{:S(2)}) %collective-permute-start.5) | collective-permute-done | bytes 1048608 | tf_op jit(solution)/shard_map/ppermute | solution.py:240
  149.8 1.0 collective-permute-start.11
  150.8 4.0 %shard_map.88.refs_4_ = f32[8,512,512]{2,1,0:T(8,128)} custom-call(bf16[512,512]{1,0:T(8,128)(2,1)S(1)} %get-tuple-element.32.refs_0_.refs_3_, bf16[512,512]{1,0:T(8,128)(2,1)S(1)} %get-tuple-element.31.refs_1_.refs_4_, f32[2,256,512]{2,1,0:T(8,128)S(1)} %shard_map.83.refs_2_, ...), custom_call_target="tpu_custom_call", output_to_operand_aliasing={{}: (4, {})} | custom-call | flops 1610612736 | bytes 4194304 | tf_op jit(solution)/shard_map/pallas_call | solution.py:106
  154.8 4.2 %shard_map.92.refs_4_ = f32[8,512,512]{2,1,0:T(8,128)} custom-call(bf16[512,512]{1,0:T(8,128)(2,1)S(1)} %get-tuple-element.32.refs_0_.refs_3_, bf16[512,512]{1,0:T(8,128)(2,1)S(1)} %get-tuple-element.31.refs_1_.refs_4_, f32[2,256,512]{2,1,0:T(8,128)} %collective-permute-done.8.refs_2_, f32[2,256,512]{2,1,0:T(8,128)} %collective-permute-done.12.refs_3_), custom_call_target="tpu_custom_call" | custom-call | flops 1610612736 | bytes 4194304 | tf_op jit(solution)/shard_map/pallas_call | solution.py:106
  159.0 3.1 %slice_bitcast_fusion.4 = (f32[512,512]{1,0:T(8,128)}, f32[512,512]{1,0:T(8,128)}) fusion(f32[8,512,512]{2,1,0:T(8,128)} %shard_map.92.refs_4_), kind=kLoop, calls=%fused_computation.12 | loop fusion | bytes 4194304 | tf_op jit(solution)/shard_map/squeeze | solution.py:308
  162.0 0.9 collective-permute-done.4.refs_3_
  162.9 2.9 %collective-permute-start.15 = (f32[512,512]{1,0:T(8,128)}, f32[512,512]{1,0:T(8,128)}, u32[]{:S(2)}, u32[]{:S(2)}) collective-permute-start(f32[512,512]{1,0:T(8,128)} %get-tuple-element.20), channel_id=1, source_target_pairs={{2,0},{4,2},{6,4},{8,6},{10,8},{12,10},{14,12},{18,16},{20,18},{22... | collective-permute-start | bytes 3145736 | tf_op jit(solution)/shard_map/ppermute | solution.py:256
  165.8 24.5 %collective-permute-done.6.refs_2_ = f32[1,256,512]{2,1,0:T(8,128)S(1)} collective-permute-done((f32[1,256,512]{2,1,0:T(8,128)S(1)}, f32[1,256,512]{2,1,0:T(8,128)S(1)}, u32[]{:S(2)}, u32[]{:S(2)}) %collective-permute-start.6) | collective-permute-done | bytes 524320 | tf_op jit(solution)/shard_map/ppermute | solution.py:240
  190.2 1.9 collective-permute-start.14
  192.2 2.6 collective-permute-start.16
  194.9 1.0 copy-done.9
  195.9 5.6 %collective-permute-start.17 = (f32[1,256,512]{2,1,0:T(8,128)}, f32[1,256,512]{2,1,0:T(8,128)S(1)}, u32[]{:S(2)}, u32[]{:S(2)}) collective-permute-start(f32[1,256,512]{2,1,0:T(8,128)} %shard_map.82.refs_2_), channel_id=1, source_target_pairs={{0,30},{2,28},{4,26},{6,24},{8,22},{10,20},{12,18},{14,16},{16,14}... | collective-permute-start | bytes 1572872 | tf_op jit(solution)/shard_map/ppermute | solution.py:240
  201.5 2.7 collective-permute-done.3.refs_3_
  204.2 0.8 copy-done.15
  205.3 1.0 copy-done.8
  206.3 1.0 copy-done.14
  207.4 2.0 shard_map.90.refs_4_
  209.4 4.1 %shard_map.93.refs_4_ = f32[8,512,512]{2,1,0:T(8,128)} custom-call(bf16[512,512]{1,0:T(8,128)(2,1)S(1)} %get-tuple-element.32.refs_0_.refs_3_, bf16[512,512]{1,0:T(8,128)(2,1)S(1)} %get-tuple-element.31.refs_1_.refs_4_, f32[2,256,512]{2,1,0:T(8,128)} %collective-permute-done.5.refs_2_, ...), custom_call_target="tpu_custom_call", output_to_operand_aliasing={{}: (4, {})} | custom-call | flops 1610612736 | bytes 4194304 | tf_op jit(solution)/shard_map/pallas_call | solution.py:106
  213.4 3.1 %shard_map.91.refs_2_.refs_3_.refs_4_ = f32[8,512,512]{2,1,0:T(8,128)} custom-call(bf16[512,512]{1,0:T(8,128)(2,1)S(1)} %get-tuple-element.32.refs_0_.refs_3_, bf16[512,512]{1,0:T(8,128)(2,1)S(1)} %get-tuple-element.31.refs_1_.refs_4_, f32[1,256,512]{2,1,0:T(8,128)} %shard_map.82.refs_2_, ...), custom_call_target="tpu_custom_call", output_to_operand_aliasing={{}: (4, {})} | custom-call | flops 805306368 | bytes 2097152 | tf_op jit(solution)/shard_map/pallas_call | solution.py:106
  216.5 5.5 %collective-permute-done.15 = f32[512,512]{1,0:T(8,128)} collective-permute-done((f32[512,512]{1,0:T(8,128)}, f32[512,512]{1,0:T(8,128)}, u32[]{:S(2)}, u32[]{:S(2)}) %collective-permute-start.15) | collective-permute-done | bytes 1048608 | tf_op jit(solution)/shard_map/ppermute | solution.py:256
  222.6 0.9 collective-permute-start.18
  223.5 9.7 %collective-permute-done.16 = f32[512,512]{1,0:T(8,128)} collective-permute-done((f32[512,512]{1,0:T(8,128)}, f32[512,512]{1,0:T(8,128)}, u32[]{:S(2)}, u32[]{:S(2)}) %collective-permute-start.16) | collective-permute-done | bytes 1048608 | tf_op jit(solution)/shard_map/ppermute | solution.py:256
  233.1 3.6 %fusion.5 = (f32[1,512,512]{2,1,0:T(8,128)S(1)}, f32[1,512,512]{2,1,0:T(8,128)S(1)}, f32[512,512]{1,0:T(8,128)S(1)}) fusion(f32[8,512,512]{2,1,0:T(8,128)} %shard_map.91.refs_2_.refs_3_.refs_4_, f32[512,512]{1,0:T(8,128)} %collective-permute-done.14, f32[512,512]{1,0:T(8,128)} %collective-permute-done.13, f32[512]{0:T(512)S(1)} %bitcast.54, ...), kind=kLoop, calls=%fused_computation.11 | loop fusion | flops 5242880 | bytes 9447432 | tf_op jit(solution)/shard_map/stack | solution.py:321
  236.9 4.3 %shard_map.94.refs_4_.refs_5_.refs_6_.refs_7_ = f32[8,512,512]{2,1,0:T(8,128)} custom-call(bf16[512,512]{1,0:T(8,128)(2,1)S(1)} %get-tuple-element.32.refs_0_.refs_3_, bf16[512,512]{1,0:T(8,128)(2,1)S(1)} %get-tuple-element.31.refs_1_.refs_4_, f32[2,256,512]{2,1,0:T(8,128)} %collective-permute-done.9.refs_2_, ...), custom_call_target="tpu_custom_call", output_to_operand_aliasing={{}: (4, {})} | custom-call | flops 1610612736 | bytes 4194304 | tf_op jit(solution)/shard_map/pallas_call | solution.py:106
  241.2 12.3 %shard_map.97.refs_13_ = f32[8,256,512]{2,1,0:T(8,128)} custom-call(f32[512,512]{1,0:T(8,128)S(1)} %get-tuple-element.30.refs_0_, f32[512,128]{1,0:T(8,128)S(1)} %pad.4.refs_1_, f32[8,512,512]{2,1,0:T(8,128)} %shard_map.91.refs_2_.refs_3_.refs_4_, f32[8,512,512]{2,1,0:T(8,128)} %shard_map.91.refs_2_.refs_3_.refs_4_, ...), custom_call_target="tpu_custom_call" | custom-call | flops 3221225472 | bytes 29360128 | tf_op jit(solution)/shard_map/pallas_call | solution.py:161
  253.5 2.0 shard_map.95.refs_5_.refs_6_.refs_7_
  255.5 9.5 %shard_map.96.refs_2_ = f32[3,512,512]{2,1,0:T(8,128)} custom-call(f32[512,512]{1,0:T(8,128)S(1)} %get-tuple-element.30.refs_0_, f32[512,128]{1,0:T(8,128)S(1)} %pad.4.refs_1_, f32[8,512,512]{2,1,0:T(8,128)} %shard_map.91.refs_2_.refs_3_.refs_4_, f32[8,512,512]{2,1,0:T(8,128)} %shard_map.91.refs_2_.refs_3_.refs_4_, ...), custom_call_target="tpu_custom_call" | custom-call | flops 9437184 | bytes 25165824 | tf_op jit(solution)/shard_map/pallas_call | solution.py:188
  265.0 5.2 %shard_map.98.refs_11_ = f32[8,256,512]{2,1,0:T(8,128)} custom-call(f32[512,512]{1,0:T(8,128)S(1)} %get-tuple-element.30.refs_0_, f32[512,128]{1,0:T(8,128)S(1)} %pad.4.refs_1_, f32[8,512,512]{2,1,0:T(8,128)} %shard_map.91.refs_2_.refs_3_.refs_4_, f32[8,512,512]{2,1,0:T(8,128)} %shard_map.91.refs_2_.refs_3_.refs_4_, ...), custom_call_target="tpu_custom_call", output_to_operand_aliasing={{}: (13, {})} | custom-call | flops 805306368 | bytes 7340032 | tf_op jit(solution)/shard_map/pallas_call | solution.py:161
  270.2 7.1 %shard_map.99 = f32[8,256,512]{2,1,0:T(8,128)} custom-call(f32[512,512]{1,0:T(8,128)S(1)} %get-tuple-element.30.refs_0_, f32[512,128]{1,0:T(8,128)S(1)} %pad.4.refs_1_, f32[3,512,512]{2,1,0:T(8,128)} %shard_map.96.refs_2_, bf16[512,512]{1,0:T(8,128)(2,1)S(1)} %get-tuple-element.32.refs_0_.refs_3_, ...), custom_call_target="tpu_custom_call", output_to_operand_aliasing={{}: (11, {})} | custom-call | flops 3221225472 | bytes 6291456 | tf_op jit(solution)/shard_map/pallas_call | solution.py:222
  (60 shorter events, 3.1 us)
Async XLA Ops:
  0.0 1.0 copy-start.1
  1.0 1.0 copy-start.3
  2.1 0.7 copy-start.17
  2.7 11.4 %copy-start.2 = (bf16[512,512]{1,0:T(8,128)(2,1)S(1)}, bf16[512,512]{1,0:T(8,128)(2,1)}, u32[]{:S(2)}) copy-start(bf16[512,512]{1,0:T(8,128)(2,1)} %constant.46.clone.high) | copy-start | bytes 1572868
  2.7 11.4 %copy-start.4 = (bf16[512,512]{1,0:T(8,128)(2,1)S(1)}, bf16[512,512]{1,0:T(8,128)(2,1)}, u32[]{:S(2)}) copy-start(bf16[512,512]{1,0:T(8,128)(2,1)} %constant.47.clone.low) | copy-start | bytes 1572868
  2.7 11.4 %copy-start.18 = (f32[4]{0:T(128)S(1)}, f32[4]{0:T(128)}, u32[]{:S(2)}) copy-start(f32[4]{0:T(128)} %volts.9) | copy-start | bytes 52
  6.1 24.3 %collective-permute-start = (f32[2,256,512]{2,1,0:T(8,128)}, f32[2,256,512]{2,1,0:T(8,128)}, u32[]{:S(2)}, u32[]{:S(2)}) collective-permute-start(f32[2,256,512]{2,1,0:T(8,128)} %shard_map.84.refs_2_), channel_id=1, source_target_pairs={{0,1},{1,0},{2,3},{3,2},{4,5},{5,4},{6,7},{7,6},{8,9},{9,8},{10,11... | collective-permute-start | bytes 3145736 | tf_op jit(solution)/shard_map/ppermute | solution.py:248
  7.3 106.1 %collective-permute-start.8 = (f32[2,256,512]{2,1,0:T(8,128)}, f32[2,256,512]{2,1,0:T(8,128)}, u32[]{:S(2)}, u32[]{:S(2)}) collective-permute-start(f32[2,256,512]{2,1,0:T(8,128)} %shard_map.84.refs_2_), channel_id=1, source_target_pairs={{0,30},{2,28},{4,26},{6,24},{8,22},{10,20},{12,18},{14,16},{16,14}... | collective-permute-start | bytes 3145736 | tf_op jit(solution)/shard_map/ppermute | solution.py:240
  13.6 105.0 %collective-permute-start.2 = (f32[2,256,512]{2,1,0:T(8,128)}, f32[2,256,512]{2,1,0:T(8,128)}, u32[]{:S(2)}, u32[]{:S(2)}) collective-permute-start(f32[2,256,512]{2,1,0:T(8,128)} %shard_map.86.refs_2_), channel_id=1, source_target_pairs={{0,1},{1,0},{2,3},{3,2},{4,5},{5,4},{6,7},{7,6},{8,9},{9,8},{10,11... | collective-permute-start | bytes 3145736 | tf_op jit(solution)/shard_map/ppermute | solution.py:248
  13.9 135.3 %collective-permute-start.5 = (f32[2,256,512]{2,1,0:T(8,128)}, f32[2,256,512]{2,1,0:T(8,128)}, u32[]{:S(2)}, u32[]{:S(2)}) collective-permute-start(f32[2,256,512]{2,1,0:T(8,128)} %shard_map.86.refs_2_), channel_id=1, source_target_pairs={{0,30},{2,28},{4,26},{6,24},{8,22},{10,20},{12,18},{14,16},{16,14}... | collective-permute-start | bytes 3145736 | tf_op jit(solution)/shard_map/ppermute | solution.py:240
  34.6 115.2 %collective-permute-start.1 = (f32[2,256,512]{2,1,0:T(8,128)S(1)}, f32[2,256,512]{2,1,0:T(8,128)}, u32[]{:S(2)}, u32[]{:S(2)}) collective-permute-start(f32[2,256,512]{2,1,0:T(8,128)S(1)} %shard_map.83.refs_2_), channel_id=1, source_target_pairs={{0,1},{1,0},{2,3},{3,2},{4,5},{5,4},{6,7},{7,6},{8,9},{9,8},{10,11... | collective-permute-start | bytes 3145736 | tf_op jit(solution)/shard_map/ppermute | solution.py:248
  113.4 36.4 %collective-permute-start.12 = (f32[2,256,512]{2,1,0:T(8,128)}, f32[2,256,512]{2,1,0:T(8,128)}, u32[]{:S(2)}, u32[]{:S(2)}) collective-permute-start(f32[2,256,512]{2,1,0:T(8,128)} %collective-permute-done.8.refs_2_), channel_id=1, source_target_pairs={{0,1},{1,0},{2,3},{3,2},{4,5},{5,4},{6,7},{7,6},{8,9},{9,8},{10,11... | collective-permute-start | bytes 3145736 | tf_op jit(solution)/shard_map/ppermute | solution.py:248
  116.7 73.5 %collective-permute-start.13 = (f32[512,512]{1,0:T(8,128)}, f32[512,512]{1,0:T(8,128)}, u32[]{:S(2)}, u32[]{:S(2)}) collective-permute-start(f32[512,512]{1,0:T(8,128)} %get-tuple-element.19), channel_id=1, source_target_pairs={{0,2},{2,4},{4,6},{6,8},{8,10},{10,12},{12,14},{16,18},{18,20},{20... | collective-permute-start | bytes 3145736 | tf_op jit(solution)/shard_map/ppermute | solution.py:255
  118.7 73.5 %collective-permute-start.9 = (f32[2,256,512]{2,1,0:T(8,128)S(1)}, f32[2,256,512]{2,1,0:T(8,128)}, u32[]{:S(2)}, u32[]{:S(2)}) collective-permute-start(f32[2,256,512]{2,1,0:T(8,128)S(1)} %shard_map.83.refs_2_), channel_id=1, source_target_pairs={{0,30},{2,28},{4,26},{6,24},{8,22},{10,20},{12,18},{14,16},{16,14}... | collective-permute-start | bytes 3145736 | tf_op jit(solution)/shard_map/ppermute | solution.py:240
  121.3 2.2 copy-start
  125.1 24.6 %copy-start.7 = (f32[1,256,512]{2,1,0:T(8,128)}, f32[1,256,512]{2,1,0:T(8,128)S(1)}, u32[]{:S(2)}) copy-start(f32[1,256,512]{2,1,0:T(8,128)S(1)} %shard_map.89.refs_2_) | copy-start | bytes 1572868
  149.2 13.7 %collective-permute-start.4 = (f32[1,256,512]{2,1,0:T(8,128)S(1)}, f32[1,256,512]{2,1,0:T(8,128)S(1)}, u32[]{:S(2)}, u32[]{:S(2)}) collective-permute-start(f32[1,256,512]{2,1,0:T(8,128)S(1)} %shard_map.89.refs_2_), channel_id=1, source_target_pairs={{0,1},{1,0},{2,3},{3,2},{4,5},{5,4},{6,7},{7,6},{8,9},{9,8},{10,11... | collective-permute-start | bytes 1572872 | tf_op jit(solution)/shard_map/ppermute | solution.py:248
  149.7 40.5 %collective-permute-start.6 = (f32[1,256,512]{2,1,0:T(8,128)S(1)}, f32[1,256,512]{2,1,0:T(8,128)S(1)}, u32[]{:S(2)}, u32[]{:S(2)}) collective-permute-start(f32[1,256,512]{2,1,0:T(8,128)S(1)} %shard_map.89.refs_2_), channel_id=1, source_target_pairs={{0,30},{2,28},{4,26},{6,24},{8,22},{10,20},{12,18},{14,16},{16,14}... | collective-permute-start | bytes 1572872 | tf_op jit(solution)/shard_map/ppermute | solution.py:240
  149.8 45.1 %collective-permute-start.11 = (f32[2,256,512]{2,1,0:T(8,128)}, f32[2,256,512]{2,1,0:T(8,128)S(1)}, u32[]{:S(2)}, u32[]{:S(2)}) collective-permute-start(f32[2,256,512]{2,1,0:T(8,128)} %collective-permute-done.5.refs_2_), channel_id=1, source_target_pairs={{0,1},{1,0},{2,3},{3,2},{4,5},{5,4},{6,7},{7,6},{8,9},{9,8},{10,11... | collective-permute-start | bytes 3145736 | tf_op jit(solution)/shard_map/ppermute | solution.py:248
  154.8 40.0 %copy-start.19 = (f32[2,512]{1,0:T(2,128)S(1)}, f32[2,512]{1,0:T(2,128)}, u32[]{:S(2)}) copy-start(f32[2,512]{1,0:T(2,128)} %param.11) | copy-start | bytes 12292
  162.9 38.6 %copy-start.13 = (f32[1,256,512]{2,1,0:T(8,128)}, f32[1,256,512]{2,1,0:T(8,128)S(1)}, u32[]{:S(2)}) copy-start(f32[1,256,512]{2,1,0:T(8,128)S(1)} %collective-permute-done.4.refs_3_) | copy-start | bytes 1572868
  162.9 59.1 %collective-permute-start.15 = (f32[512,512]{1,0:T(8,128)}, f32[512,512]{1,0:T(8,128)}, u32[]{:S(2)}, u32[]{:S(2)}) collective-permute-start(f32[512,512]{1,0:T(8,128)} %get-tuple-element.20), channel_id=1, source_target_pairs={{2,0},{4,2},{6,4},{8,6},{10,8},{12,10},{14,12},{18,16},{20,18},{22... | collective-permute-start | bytes 3145736 | tf_op jit(solution)/shard_map/ppermute | solution.py:256
  190.2 4.7 %copy-start.11 = (f32[1,256,512]{2,1,0:T(8,128)}, f32[1,256,512]{2,1,0:T(8,128)S(1)}, u32[]{:S(2)}) copy-start(f32[1,256,512]{2,1,0:T(8,128)S(1)} %collective-permute-done.6.refs_2_) | copy-start | bytes 1572868
  190.2 13.9 %collective-permute-start.3 = (f32[1,256,512]{2,1,0:T(8,128)}, f32[1,256,512]{2,1,0:T(8,128)S(1)}, u32[]{:S(2)}, u32[]{:S(2)}) collective-permute-start(f32[1,256,512]{2,1,0:T(8,128)} %shard_map.82.refs_2_), channel_id=1, source_target_pairs={{0,1},{1,0},{2,3},{3,2},{4,5},{5,4},{6,7},{7,6},{8,9},{9,8},{10,11... | collective-permute-start | bytes 1572872 | tf_op jit(solution)/shard_map/ppermute | solution.py:248
  190.2 33.2 %collective-permute-start.14 = (f32[512,512]{1,0:T(8,128)}, f32[512,512]{1,0:T(8,128)}, u32[]{:S(2)}, u32[]{:S(2)}) collective-permute-start(f32[512,512]{1,0:T(8,128)} %get-tuple-element.21), channel_id=1, source_target_pairs={{0,2},{2,4},{4,6},{6,8},{8,10},{10,12},{12,14},{16,18},{18,20},{20... | collective-permute-start | bytes 3145736 | tf_op jit(solution)/shard_map/ppermute | solution.py:255
  192.2 41.0 %collective-permute-start.16 = (f32[512,512]{1,0:T(8,128)}, f32[512,512]{1,0:T(8,128)}, u32[]{:S(2)}, u32[]{:S(2)}) collective-permute-start(f32[512,512]{1,0:T(8,128)} %get-tuple-element.22), channel_id=1, source_target_pairs={{2,0},{4,2},{6,4},{8,6},{10,8},{12,10},{14,12},{18,16},{20,18},{22... | collective-permute-start | bytes 3145736 | tf_op jit(solution)/shard_map/ppermute | solution.py:256
  194.9 1.0 copy-start.9
  195.9 26.7 %collective-permute-start.17 = (f32[1,256,512]{2,1,0:T(8,128)}, f32[1,256,512]{2,1,0:T(8,128)S(1)}, u32[]{:S(2)}, u32[]{:S(2)}) collective-permute-start(f32[1,256,512]{2,1,0:T(8,128)} %shard_map.82.refs_2_), channel_id=1, source_target_pairs={{0,30},{2,28},{4,26},{6,24},{8,22},{10,20},{12,18},{14,16},{16,14}... | collective-permute-start | bytes 1572872 | tf_op jit(solution)/shard_map/ppermute | solution.py:240
  204.2 0.8 copy-start.15
  205.0 31.9 %collective-permute-start.10 = (f32[2,256,512]{2,1,0:T(8,128)}, f32[2,256,512]{2,1,0:T(8,128)}, u32[]{:S(2)}, u32[]{:S(2)}) collective-permute-start(f32[2,256,512]{2,1,0:T(8,128)} %collective-permute-done.9.refs_2_), channel_id=1, source_target_pairs={{0,1},{1,0},{2,3},{3,2},{4,5},{5,4},{6,7},{7,6},{8,9},{9,8},{10,11... | collective-permute-start | bytes 3145736 | tf_op jit(solution)/shard_map/ppermute | solution.py:248
  205.3 1.0 copy-start.8
  206.3 1.0 copy-start.14
  207.4 2.0 copy-start.10
  209.4 4.1 %copy-start.16 = (f32[1,256,512]{2,1,0:T(8,128)S(1)}, f32[1,256,512]{2,1,0:T(8,128)}, u32[]{:S(2)}) copy-start(f32[1,256,512]{2,1,0:T(8,128)} %copy-done.15) | copy-start | bytes 1572868
  213.4 8.6 %copy-start.12 = (f32[1,256,512]{2,1,0:T(8,128)S(1)}, f32[1,256,512]{2,1,0:T(8,128)}, u32[]{:S(2)}) copy-start(f32[1,256,512]{2,1,0:T(8,128)} %copy-done.11) | copy-start | bytes 1572868
  222.0 31.5 %collective-permute-start.7 = (f32[1,256,512]{2,1,0:T(8,128)S(1)}, f32[1,256,512]{2,1,0:T(8,128)S(1)}, u32[]{:S(2)}, u32[]{:S(2)}) collective-permute-start(f32[1,256,512]{2,1,0:T(8,128)S(1)} %copy-done.12), channel_id=1, source_target_pairs={{0,1},{1,0},{2,3},{3,2},{4,5},{5,4},{6,7},{7,6},{8,9},{9,8},{10,11... | collective-permute-start | bytes 1572872 | tf_op jit(solution)/shard_map/ppermute | solution.py:248
  222.6 47.6 %collective-permute-start.18 = (f32[1,256,512]{2,1,0:T(8,128)S(1)}, f32[1,256,512]{2,1,0:T(8,128)S(1)}, u32[]{:S(2)}, u32[]{:S(2)}) collective-permute-start(f32[1,256,512]{2,1,0:T(8,128)S(1)} %collective-permute-done.17.refs_5_), channel_id=1, source_target_pairs={{0,1},{1,0},{2,3},{3,2},{4,5},{5,4},{6,7},{7,6},{8,9},{9,8},{10,11... | collective-permute-start | bytes 1572872 | tf_op jit(solution)/shard_map/ppermute | solution.py:248
  236.9 4.3 %copy-start.5 = (bf16[512,512]{1,0:T(8,128)(2,1)S(1)}, bf16[512,512]{1,0:T(8,128)(2,1)}, u32[]{:S(2)}) copy-start(bf16[512,512]{1,0:T(8,128)(2,1)} %constant.48.clone.refs_11_.refs_9_) | copy-start | bytes 1572868
  236.9 4.3 %copy-start.6 = (bf16[512,512]{1,0:T(8,128)(2,1)S(1)}, bf16[512,512]{1,0:T(8,128)(2,1)}, u32[]{:S(2)}) copy-start(bf16[512,512]{1,0:T(8,128)(2,1)} %constant.49.clone.refs_12_.refs_10_) | copy-start | bytes 1572868

commit v2 on v0

v2 whole, which is shorter than its diff:
```python
import functools

import jax
import jax.numpy as jnp
import ml_dtypes
import numpy as np
from jax import lax
from jax.experimental import pallas as pl
from jax.experimental.pallas import tpu as pltpu
from jax.sharding import PartitionSpec as P

NX = 512
NY = 512
F32 = jnp.float32
BF16 = jnp.bfloat16
VMEM_LIMIT = 60 * 1024 * 1024


def table_parts():
    f = np.float32
    index = np.arange(NX, dtype=f) + f(1)
    inverse = f(1) / f(NX + 1)
    angle = ((f(np.pi) * index[:, None]) * index[None, :]) * inverse
    basis = np.sqrt(f(2) / f(NX + 1)).astype(f) * np.sin(angle.astype(np.float64)).astype(f)
    high = basis.astype(ml_dtypes.bfloat16)
    low = (basis - high.astype(f)).astype(ml_dtypes.bfloat16)
    return high, low


BASIS = table_parts()
BASIS_T = tuple(np.ascontiguousarray(part.T) for part in BASIS)


def split(x):
    high = x.astype(BF16)
    return high, (x - high.astype(F32)).astype(BF16)


def dot3(left, right):
    def dot(a, b):
        return jnp.dot(a, b, preferred_element_type=F32)

    return dot(left[0], right[0]) + (dot(left[0], right[1]) + dot(left[1], right[0]))


def after(value, *others):
    return lax.optimization_barrier((value,) + others)[0]


def whole(shape):
    return pl.BlockSpec(shape, lambda g: (0,) * len(shape))


def call(body, grid, in_specs, out_specs, out_shape, cost, scratch=(), aliases=None):
    return pl.pallas_call(
        body,
        grid=(grid,),
        in_specs=in_specs,
        out_specs=out_specs,
        out_shape=out_shape,
        scratch_shapes=scratch,
        input_output_aliases=aliases or {},
        compiler_params=pltpu.CompilerParams(
            dimension_semantics=("arbitrary",), vmem_limit_bytes=VMEM_LIMIT
        ),
        cost_estimate=pl.CostEstimate(flops=cost[0], bytes_accessed=cost[1], transcendentals=0),
    )


COST = {
    "rows": (1, 1),
    "modes": (1, 1),
    "own": (1, 1),
    "first": (1, 1),
    "next": (1, 1),
    "step": (1, 1),
    "base": (1, 1),
    "last": (1, 1),
}


def halves(refs):
    return tuple(ref[...] for ref in refs)


def joined(refs):
    return split(jnp.concatenate([ref[...] for ref in refs], axis=0))


def row_modes(source, labels, voltages, planes, uses):
    rows = source.shape[1]
    first, stride = planes[0], planes[1] - planes[0]
    count = len(planes)

    def body(volts, source_ref, labels_ref, high, low, *outs):
        label = labels_ref[...]
        pick = jnp.full(label.shape, volts[0], F32)
        for region in range(1, volts.shape[0]):
            pick = jnp.where(label == region, volts[region], pick)
        modes = dot3(split(source_ref[...] + pick), (high[...], low[...]))
        g = pl.program_id(0)
        for use, out in zip(uses, outs):
            start = planes.index(use[0])
            if len(use) == count:
                out[...] = modes
            else:
                pl.when((g >= start) & (g < start + len(use)))(functools.partial(put, out, modes))

    block = pl.BlockSpec((None, rows, NY), lambda g: (first + stride * g, 0, 0))

    def slot(use):
        start, last = planes.index(use[0]), len(use) - 1
        return pl.BlockSpec((None, rows, NY), lambda g: (jnp.clip(g - start, 0, last), 0, 0))

    return call(
        body,
        count,
        [pl.BlockSpec(memory_space=pltpu.SMEM), block, block, whole((NY, NY)), whole((NY, NY))],
        [slot(use) for use in uses],
        [jax.ShapeDtypeStruct((len(use), rows, NY), F32) for use in uses],
        COST["rows"],
    )(voltages, source, labels, *[jnp.asarray(part) for part in BASIS_T])


def put(out, value):
    out[...] = value


def own_part(flags, inverse, weights, table, ends, others):
    count = len(ends)
    rows = ends[0].shape[1]
    total = 2 + others[0].shape[0]

    def stack(slots, slot):
        return [pl.BlockSpec((None, rows, NY), lambda g: (jnp.clip(slot(g), 0, slots - 1), 0, 0))] * count

    def body(flag, inv_ref, wts, *refs):
        th, tl = refs[:2]
        end_refs, other_refs = refs[2:2 + count], refs[2 + count:2 + 2 * count]
        out, first_out, last_out, ring = refs[2 + 2 * count:]
        g = pl.program_id(0)

        def load(group):
            ring[lax.rem(g, 3)] = dot3(halves((th, tl)), joined(group))

        pl.when((g == 0) | (g == total - 1))(lambda: load(end_refs))
        pl.when((g > 0) & (g < total - 1))(lambda: load(other_refs))

        @pl.when(g == 0)
        def _():
            first_out[...] = ring[0]

        @pl.when(g == total - 1)
        def _():
            last_out[...] = ring[(total - 1) % 3]

        @pl.when(g > 0)
        def _():
            plane = g - 1
            bottom, top = plane == 0, plane == total - 1
            mid, inv = ring[lax.rem(plane, 3)], inv_ref[...]
            below = jnp.where(bottom, 0.0, ring[lax.rem(plane + 2, 3)])
            above = jnp.where(top, 0.0, ring[lax.rem(plane + 1, 3)])
            turn = jnp.where(bottom, flag[0], 0.0) - jnp.where(top, flag[1], 0.0)
            far = wts[:, 2:3] * (below + above) + (turn * wts[:, 4:5]) * mid
            out[...] = inv * (wts[:, 0:1] * mid + inv * far)

    return call(
        body,
        total + 1,
        [pl.BlockSpec(memory_space=pltpu.SMEM), whole((NX, NY)), whole((NX, 128))]
        + [whole((NX, NX))] * 2
        + stack(2, lambda g: jnp.where(g > 0, 1, 0))
        + stack(total - 2, lambda g: total - 2 - g),
        [
            pl.BlockSpec((None, NX, NY), lambda g: (jnp.maximum(g - 1, 0), 0, 0)),
            whole((NX, NY)),
            whole((NX, NY)),
        ],
        [
            jax.ShapeDtypeStruct((total, NX, NY), F32),
            jax.ShapeDtypeStruct((NX, NY), F32),
            jax.ShapeDtypeStruct((NX, NY), F32),
        ],
        COST["own"],
        scratch=[pltpu.VMEM((3, NX, NY), F32)],
    )(flags, inverse, weights, *table, *ends, *others)


def part_specs(parts, slot):
    return [pl.BlockSpec((None,) + part.shape[1:], lambda g: (slot, 0, 0)) for part in parts]


def first_planes(inverse, weights, x_table, outer, inner, partial, own_first, own_last, rows_table, table):
    count, total, rows = len(outer), partial.shape[0], rows_table[0].shape[0]

    def body(*refs):
        inv, wts = refs[:2]
        outer_refs, inner_refs = refs[4:4 + count], refs[4 + count:4 + 2 * count]
        part, first_ref, last_ref = refs[4 + 2 * count:7 + 2 * count]
        near_rows, grid_table = refs[7 + 2 * count:9 + 2 * count], refs[9 + 2 * count:11 + 2 * count]
        top, plane_0, plane_1, plane_2, to_above, to_below, out = refs[-7:]
        g = pl.program_id(0)

        def fill(target, group):
            target[...] = dot3(halves(refs[2:4]), joined(group))

        @pl.when(g == 0)
        def _():
            fill(top, outer_refs)
            to_above[...] = wts[:, 2:3] * last_ref[...] + wts[:, 3:4] * top[...]

        @pl.when(g == 1)
        def _():
            fill(plane_0, outer_refs)
            to_below[...] = wts[:, 2:3] * first_ref[...] + wts[:, 3:4] * plane_0[...]

        @pl.when(g == 2)
        def _():
            fill(plane_1, inner_refs)

        @pl.when(g == 3)
        def _():
            fill(plane_2, inner_refs)
            modes = part[...] + other_part(inv[...], wts, plane_0[...], plane_1[...], plane_2[...])
            out[...] = dot3(split(dot3(halves(near_rows), split(modes))), halves(grid_table))

    stack = (None,) + outer[0].shape[1:]
    return call(
        body,
        4,
        [whole((NX, NY)), whole((NX, 128))] + [whole((NX, NX))] * 2
        + [pl.BlockSpec(stack, lambda g: (jnp.minimum(g, 1), 0, 0))] * count
        + [pl.BlockSpec(stack, lambda g: (jnp.maximum(g - 2, 0), 0, 0))] * count
        + [pl.BlockSpec((None, NX, NY), lambda g: (1, 0, 0))] + [whole((NX, NY))] * 2
        + [whole((rows, NX))] * 2 + [whole((NY, NY))] * 2,
        [whole((NX, NY))] * 6 + [pl.BlockSpec((None, rows, NY), lambda g: (1, 0, 0))],
        [jax.ShapeDtypeStruct((NX, NY), F32)] * 6 + [jax.ShapeDtypeStruct((total, rows, NY), F32)],
        COST["first"],
    )(inverse, weights, *x_table, *outer, *inner, partial, own_first, own_last, *rows_table, *table)


def next_planes(inverse, weights, x_table, parts, partial, place, low, mid, rows_table, table, buffer):
    count, total, rows = len(parts), partial.shape[0], rows_table[0].shape[0]

    def body(*refs):
        inv, wts = refs[:2]
        part, low_ref, mid_ref = refs[4 + count:7 + count]
        near_rows, grid_table = refs[7 + count:9 + count], refs[9 + count:11 + count]
        high_out, higher_out, out = refs[-3:]
        g = pl.program_id(0)

        def finish(target, *planes):
            target[...] = dot3(halves(refs[2:4]), joined(refs[4:4 + count]))
            modes = part[...] + other_part(inv[...], wts, *[plane[...] for plane in planes], target[...])
            out[...] = dot3(split(dot3(halves(near_rows), split(modes))), halves(grid_table))

        pl.when(g == 0)(lambda: finish(high_out, low_ref, mid_ref))
        pl.when(g == 1)(lambda: finish(higher_out, mid_ref, high_out))

    return call(
        body,
        2,
        [whole((NX, NY)), whole((NX, 128))] + [whole((NX, NX))] * 2
        + [pl.BlockSpec((None,) + parts[0].shape[1:], lambda g: (g, 0, 0))] * count
        + [pl.BlockSpec((None, NX, NY), lambda g: (place + g, 0, 0))] + [whole((NX, NY))] * 2
        + [whole((rows, NX))] * 2 + [whole((NY, NY))] * 2 + [pl.BlockSpec(memory_space=pl.ANY)],
        [whole((NX, NY))] * 2 + [pl.BlockSpec((None, rows, NY), lambda g: (place + g, 0, 0))],
        [jax.ShapeDtypeStruct((NX, NY), F32)] * 2 + [jax.ShapeDtypeStruct((total, rows, NY), F32)],
        COST["next"],
        aliases={11 + count: 2},
    )(inverse, weights, *x_table, *parts, partial, low, mid, *rows_table, *table, buffer)


def end_plane(inverse, weights, partial, mid, high, edge, rows_table, table, buffer):
    rows = rows_table[0].shape[0]

    def body(inv_ref, wts, part, mid_ref, high_ref, edge_ref, *refs):
        inv = inv_ref[...]
        modes = part[...] + other_part(inv, wts, None, mid_ref[...], high_ref[...]) + inv * inv * edge_ref[...]
        refs[-1][...] = dot3(split(dot3(halves(refs[:2]), split(modes))), halves(refs[2:4]))

    return call(
        body,
        1,
        [whole((NX, NY)), whole((NX, 128)), pl.BlockSpec((None, NX, NY), lambda g: (0, 0, 0))]
        + [whole((NX, NY))] * 3 + [whole((rows, NX))] * 2 + [whole((NY, NY))] * 2
        + [pl.BlockSpec(memory_space=pl.ANY)],
        pl.BlockSpec((None, rows, NY), lambda g: (0, 0, 0)),
        jax.ShapeDtypeStruct(buffer.shape, F32),
        COST["step"],
        aliases={10: 0},
    )(inverse, weights, partial, mid, high, edge, *rows_table, *table, buffer)


def other_part(inv, wts, low, mid, high):
    far = low if high is None else high if low is None else low + high
    return inv * (wts[:, 1:2] * mid + inv * (wts[:, 3:4] * far))


def step(inverse, weights, x_table, parts, slot, partial, place, low, mid, rows_table, table, buffer):
    total, rows, count = partial.shape[0], rows_table[0].shape[0], len(parts)
    aliased = 0 if buffer is None else 1

    def body(*refs):
        inv, wts = refs[:2]
        part, low_ref, mid_ref = refs[4 + count:7 + count]
        near_rows, grid_table = refs[7 + count:9 + count], refs[9 + count:11 + count]
        high_out, out = refs[-2:]
        high = dot3(halves(refs[2:4]), joined(refs[4:4 + count]))
        high_out[...] = high
        modes = part[...] + other_part(inv[...], wts, low_ref[...], mid_ref[...], high)
        out[...] = dot3(split(dot3(halves(near_rows), split(modes))), halves(grid_table))

    return call(
        body,
        1,
        [whole((NX, NY)), whole((NX, 128))] + [whole((NX, NX))] * 2 + part_specs(parts, slot)
        + [pl.BlockSpec((None, NX, NY), lambda g: (place, 0, 0))] + [whole((NX, NY))] * 2
        + [whole((rows, NX))] * 2 + [whole((NY, NY))] * 2 + [pl.BlockSpec(memory_space=pl.ANY)] * aliased,
        [whole((NX, NY)), pl.BlockSpec((None, rows, NY), lambda g: (place, 0, 0))],
        [jax.ShapeDtypeStruct((NX, NY), F32), jax.ShapeDtypeStruct((total, rows, NY), F32)],
        COST["step"],
        aliases={11 + count: 1} if aliased else None,
    )(inverse, weights, *x_table, *parts, partial, low, mid, *rows_table, *table, *([buffer] if aliased else []))


def last_planes(inverse, weights, partial, x_table, parts, before, early, top, edge, rows_table, table, buffer):
    total, rows = buffer.shape[0], buffer.shape[1]
    count = len(parts)

    def body(*refs):
        inv_ref, wts, part = refs[:3]
        before_ref, early_ref, top_ref, edge_ref = refs[5 + count:9 + count]
        near_rows, grid_table = refs[9 + count:11 + count], refs[11 + count:13 + count]
        out, late = refs[-2:]
        g = pl.program_id(0)

        def finish(low, mid, high, edge=None):
            inv = inv_ref[...]
            far = wts[:, 3:4] * (low[...] if high is None else low[...] + high[...])
            if edge is not None:
                far = far + edge[...]
            modes = part[...] + inv * (wts[:, 1:2] * mid[...] + inv * far)
            out[...] = dot3(split(dot3(halves(near_rows), split(modes))), halves(grid_table))

        @pl.when(g == 0)
        def _():
            late[...] = dot3(halves(refs[3:5]), joined(refs[5:5 + count]))
            finish(before_ref, early_ref, late)

        pl.when(g == 1)(lambda: finish(early_ref, late, top_ref))
        pl.when(g == 2)(lambda: finish(late, top_ref, None, edge_ref))

    return call(
        body,
        3,
        [whole((NX, NY)), whole((NX, 128)), pl.BlockSpec((None, NX, NY), lambda g: (total - 3 + g, 0, 0))]
        + [whole((NX, NX))] * 2 + part_specs(parts, 0) + [whole((NX, NY))] * 4
        + [whole((rows, NX))] * 2 + [whole((NY, NY))] * 2 + [pl.BlockSpec(memory_space=pl.ANY)],
        pl.BlockSpec((None, rows, NY), lambda g: (total - 3 + g, 0, 0)),
        jax.ShapeDtypeStruct((total, rows, NY), F32),
        COST["last"],
        scratch=[pltpu.VMEM((NX, NY), F32)],
        aliases={13 + count: 0},
    )(inverse, weights, partial, *x_table, *parts, before, early, top, edge, *rows_table, *table, buffer)


def to_mirror(block):
    count = lax.axis_size("axial")
    return lax.ppermute(block, "axial", [(i, count - 1 - i) for i in range(count)])


def gather_rows(block):
    count = lax.axis_size("trans")
    parts = [block]
    for step in range(1, count):
        route = [(i, (i - step) % count) for i in range(count)]
        parts.append(lax.ppermute(block, "trans", route))
    return parts


def halo(first, last):
    count = lax.axis_size("axial")
    up = [(i, i + 1) for i in range(count - 1) if i + 1 != count // 2]
    below = lax.ppermute(last, "axial", up)
    above = lax.ppermute(first, "axial", [(j, i) for i, j in up])
    return below, above


def on_device(source, labels, voltages, relax):
    planes, rows = source.shape[0], source.shape[1]
    half, end = planes // 2, planes - 1
    ax_count = lax.axis_size("axial")
    position = lax.axis_index("axial")
    row_start = lax.axis_index("trans") * rows

    inner = list(range(end - 1, 0, -1))
    chunks = [[0, end], inner[:2], inner[2:4]] + [[plane] for plane in inner[4:]]
    (ends,) = row_modes(source, labels, voltages, [0, end], [[0, end]])
    others, *rest = row_modes(source, labels, after(voltages, ends), inner, [inner] + chunks[1:])
    ends, others = gather_rows(ends), gather_rows(others)
    sent = []
    for number, block in enumerate([ends[0]] + rest):
        if number < 3:
            sent.append(to_mirror(block))

    x_table = tuple(
        lax.dynamic_slice_in_dim(jnp.concatenate([part, part], axis=1), row_start, NX, 1)
        for part in (jnp.asarray(BASIS[0]), jnp.asarray(BASIS[1]))
    )
    rows_table = tuple(
        lax.dynamic_slice_in_dim(jnp.asarray(part), row_start, rows, 0) for part in BASIS_T
    )
    table = tuple(jnp.asarray(part) for part in BASIS)

    index = jnp.arange(NX, dtype=F32) + 1.0
    eigen = 2.0 - 2.0 * jnp.cos(jnp.pi * index / (NX + 1.0))
    inverse = 1.0 / (eigen[:, None] + eigen[None, :] + 2.0)
    even, odd = relax[0], relax[1]
    a_even, a_odd = (2.0 - even) * even, (2.0 - odd) * odd
    b_even, b_odd = even * even, odd * odd
    columns = [
        0.5 * (a_even + a_odd),
        0.5 * (a_even - a_odd),
        0.5 * (b_even + b_odd),
        0.5 * (b_even - b_odd),
        even * odd,
    ]
    weights = jnp.pad(jnp.stack(columns, axis=1), ((0, 0), (0, 128 - len(columns))))
    flags = jnp.stack([position == ax_count // 2, position == ax_count // 2 - 1]).astype(F32)

    passed = [gather_rows(after(sent[0], *x_table, *rows_table, inverse, weights, flags))]
    partial, own_first, own_last = own_part(flags, inverse, weights, x_table, ends, others)
    passed.append(gather_rows(sent[1]))
    sent += [to_mirror(after(block, passed[1][-1], partial)) for block in rest[2:]]
    passed.append(gather_rows(after(sent[2], partial)))
    top, plane_0, low, mid, to_above, to_below, out = first_planes(
        inverse, weights, x_table, [after(passed[0][0], sent[2])] + passed[0][1:], passed[1],
        partial, own_first, own_last, rows_table, table,
    )
    plane_1 = low
    passed.append(gather_rows(after(sent[-2], out)))
    for number in range(2, len(sent) - 2):
        low, mid, out = next_planes(
            inverse, weights, x_table, passed[number], partial, 2 * number - 2, low, mid, rows_table, table, out
        )
    below, above = halo(after(to_below, sent[-1]), after(to_above, sent[-1]))
    final = gather_rows(sent[-1])
    high, out = step(
        inverse, weights, x_table, [after(passed[-1][0], sent[-1])] + passed[-1][1:], 0,
        partial, planes - 4, low, mid, rows_table, table, out,
    )
    low, mid = mid, high
    out = end_plane(inverse, weights, partial, plane_0, plane_1, below, rows_table, table, out)
    return last_planes(
        inverse, weights, partial, x_table, final, low, mid, top, above, rows_table, table, out
    )


def solution(mesh):
    placed = (P("axial", "trans", None), P("axial", "trans", None), P(), P())
    return jax.shard_map(
        on_device, mesh=mesh, in_specs=placed, out_specs=P("axial", "trans", None), check_vma=False
    )
```

time: 1100 us -> 239 us (0.22)
  waiting for transfers between devices: 957 us -> 138 us
  matrix products: 72.8 us -> 0 us
  Pallas kernels: 0 us -> 72.1 us
  other arithmetic: 21.5 us -> 1.93 us
  between operations: 13.5 us -> 0.15 us
  local copies, waits for them, and re-layouts: 19.4 us -> 6.16 us
    ppermute x10 -> x14, waiting for transfers between devices: 758 us -> 138 us  [the longest x5 135 us: to_mirror(): lax.ppermute(block, 'axial', [(i, count - 1 - i) for i in range(count)])]
    psum x1 -> x0, waiting for transfers between devices: 199 us -> none  [on_device(): lax.psum(jnp.einsum('kx,zxj->kzj', columns, inner, precision=high), 'trans')]
    dot_general x4 -> x0, matrix products: 72.8 us -> none  [the longest x1 40 us: on_device(): back = jnp.einsum('kzj,jy->kzy', second, basis_y, precision=high)]
    pallas_call x0 -> x8, Pallas kernels: none -> 72.1 us  [the longest x1 17 us: own_part(): call(body, total + 1, [pl.BlockSpec(memory_space=pltpu.SMEM), whole((NX,...]
    add x4 -> x0, other arithmetic: 13 us -> none  [the longest x1 6.87 us: on_device(): charge = charge + jnp.where(labels == region, voltages[region], 0.0)]
  transfers between devices with their start and end apart: 11 -> 14, of which waited for: 11 -> 6; matrix products, arithmetic and copies ran while one was open for 0% -> 3% of each run, Pallas kernels for 0% -> 21%
where the time goes in v2:
time: 239 us; the launch traced here: 237 us
  waiting for transfers between devices  138 us (58%)
  Pallas kernels  72.1 us (30%)
  starting transfers between devices  19.4 us (8%)
  local copies, waits for them, and re-layouts  6.16 us (3%)
    ppermute x5, waiting for transfers between devices, to_mirror(): lax.ppermute(block, 'axial', [(i, count - 1 - i) for i in range(count)])  135 us
    pallas_call x1, Pallas kernels, own_part(): call(body, total + 1, [pl.BlockSpec(memory_space=pltpu.SMEM), whole((NX,...  17 us
    pallas_call x2, Pallas kernels, row_modes(): call(body, count, [pl.BlockSpec(memory_space=pltpu.SMEM), block, block, w...  12.6 us
    pallas_call x1, Pallas kernels, first_planes(): call(body, 4, [whole((NX, NY)), whole((NX, 128))] + [whole((NX, NX))] * 2...  12.1 us
    ppermute x5, starting transfers between devices, to_mirror(): lax.ppermute(block, 'axial', [(i, count - 1 - i) for i in range(count)])  11.2 us
    pallas_call x1, Pallas kernels, last_planes(): call(body, 3, [whole((NX, NY)), whole((NX, 128)), pl.BlockSpec((None, NX,...  9.68 us
    pallas_call x1, Pallas kernels, next_planes(): call(body, 2, [whole((NX, NY)), whole((NX, 128))] + [whole((NX, NX))] * 2...  9.29 us
    pallas_call x1, Pallas kernels, step(): call(body, 1, [whole((NX, NY)), whole((NX, 128))] + [whole((NX, NX))] * 2...  6.22 us
  transfers between devices with their start and end apart: 14, of which 6 were waited for; matrix products, arithmetic and copies ran while one was open for 3% of the time, Pallas kernels for 21%

profile of v2, /device:TPU:9, one launch (start us, length us, event | category | flops | bytes accessed | tf_op | source)
XLA Modules:
  0.0 237.4 jit_solution(11554656818077431446)
XLA Ops:
  0.0 3.6 %shard_map.82.refs_2_ = f32[2,256,512]{2,1,0:T(8,128)} custom-call(f32[4]{0:T(128)} %volts.2, f32[8,256,512]{2,1,0:T(8,128)} %source_ref.3, s32[8,256,512]{2,1,0:T(8,128)} %labels_ref.3, bf16[512,512]{1,0:T(8,128)(2,1)} %constant.44.clone.high, bf16[512,512]{1,0:T(8,128)(2,1)} %constant.45.clone.low), custom_call_target="tpu_custom_call" | custom-call | flops 1 | bytes 1 | tf_op jit(solution)/shard_map/pallas_call | solution.py:115
  3.6 0.0 copy-start.2
  3.6 0.0 copy-start.8
  3.6 9.1 %shard_map.83 = (f32[6,256,512]{2,1,0:T(8,128)}, f32[2,256,512]{2,1,0:T(8,128)}, f32[2,256,512]{2,1,0:T(8,128)}, f32[1,256,512]{2,1,0:T(8,128)}, f32[1,256,512]{2,1,0:T(8,128)}) custom-call(f32[4]{0:T(128)} %volts.2, f32[8,256,512]{2,1,0:T(8,128)} %source_ref.3, s32[8,256,512]{2,1,0:T(8,128)} %labels_ref.3, bf16[512,512]{1,0:T(8,128)(2,1)} %constant.44.clone.high, ...), custom_call_target="tpu_custom_call" | custom-call | flops 1 | bytes 1 | tf_op jit(solution)/shard_map/pallas_call | solution.py:115
  12.7 1.2 collective-permute-start.1
  13.9 3.1 %collective-permute-start.2 = (f32[2,256,512]{2,1,0:T(8,128)}, f32[2,256,512]{2,1,0:T(8,128)}, u32[]{:S(2)}, u32[]{:S(2)}) collective-permute-start(f32[2,256,512]{2,1,0:T(8,128)} %get-tuple-element.39), channel_id=1, source_target_pairs={{0,30},{2,28},{4,26},{6,24},{8,22},{10,20},{12,18},{14,16},{16,14}... | collective-permute-start | bytes 3145736 | tf_op jit(solution)/shard_map/ppermute | solution.py:371
  17.0 0.0 collective-permute-start.8
  17.0 0.3 collective-permute-start
  17.3 2.9 %collective-permute-start.6 = (f32[2,256,512]{2,1,0:T(8,128)}, f32[2,256,512]{2,1,0:T(8,128)S(1)}, u32[]{:S(2)}, u32[]{:S(2)}) collective-permute-start(f32[2,256,512]{2,1,0:T(8,128)} %get-tuple-element.41), channel_id=1, source_target_pairs={{0,30},{2,28},{4,26},{6,24},{8,22},{10,20},{12,18},{14,16},{16,14}... | collective-permute-start | bytes 3145736 | tf_op jit(solution)/shard_map/ppermute | solution.py:371
  20.2 0.0 copy-done.2
  20.2 0.9 constant_dynamic-slice_fusion
  21.1 2.3 constant_dynamic-slice_fusion.2
  23.4 85.3 %collective-permute-done.2.refs_6_ = f32[2,256,512]{2,1,0:T(8,128)} collective-permute-done((f32[2,256,512]{2,1,0:T(8,128)}, f32[2,256,512]{2,1,0:T(8,128)}, u32[]{:S(2)}, u32[]{:S(2)}) %collective-permute-start.2) | collective-permute-done | bytes 1048608 | tf_op jit(solution)/shard_map/ppermute | solution.py:371
  108.7 0.3 collective-permute-start.3
  109.0 0.6 add_convert_fusion.flag
  109.6 1.2 add_divide_fusion.inv_ref.refs_0_
  110.9 0.1 copy.23
  111.0 0.7 pad.4.wts.refs_1_
  111.8 19.3 %collective-permute-done.8.refs_4_ = f32[2,256,512]{2,1,0:T(8,128)} collective-permute-done((f32[2,256,512]{2,1,0:T(8,128)S(1)}, f32[2,256,512]{2,1,0:T(8,128)}, u32[]{:S(2)}, u32[]{:S(2)}) %collective-permute-start.8) | collective-permute-done | bytes 1048608 | tf_op jit(solution)/shard_map/ppermute | solution.py:371
  131.1 0.3 collective-permute-start.9
  131.3 0.0 collective-permute-done.refs_3_
  131.3 0.0 collective-permute-done.1.refs_5_
  131.3 17.0 %shard_map.84 = (f32[8,512,512]{2,1,0:T(8,128)}, f32[512,512]{1,0:T(8,128)}, f32[512,512]{1,0:T(8,128)}) custom-call(f32[2]{0:T(128)} %add_convert_fusion.flag, f32[512,512]{1,0:T(8,128)} %add_divide_fusion.inv_ref.refs_0_, f32[512,128]{1,0:T(8,128)} %pad.4.wts.refs_1_, bf16[512,512]{1,0:T(8,128)(2,1)} %get-tuple-element.71.refs_0_.refs_2_.refs_3_, ...), custom_call_target="tpu_custom_call" | custom-call | flops 1 | bytes 1 | tf_op jit(solution)/shard_map/pallas_call | solution.py:168
  148.3 0.0 collective-permute-done.3.refs_7_
  148.3 2.8 %collective-permute-start.4 = (f32[1,256,512]{2,1,0:T(8,128)}, f32[1,256,512]{2,1,0:T(8,128)S(1)}, u32[]{:S(2)}, u32[]{:S(2)}) collective-permute-start(f32[1,256,512]{2,1,0:T(8,128)} %get-tuple-element.40), channel_id=1, source_target_pairs={{0,30},{2,28},{4,26},{6,24},{8,22},{10,20},{12,18},{14,16},{16,14}... | collective-permute-start | bytes 1572872 | tf_op jit(solution)/shard_map/ppermute | solution.py:371
  151.1 24.9 %collective-permute-done.6.refs_4_ = f32[2,256,512]{2,1,0:T(8,128)S(1)} collective-permute-done((f32[2,256,512]{2,1,0:T(8,128)}, f32[2,256,512]{2,1,0:T(8,128)S(1)}, u32[]{:S(2)}, u32[]{:S(2)}) %collective-permute-start.6) | collective-permute-done | bytes 1048608 | tf_op jit(solution)/shard_map/ppermute | solution.py:371
  176.0 2.3 collective-permute-start.10
  178.4 0.3 collective-permute-start.7
  178.6 0.0 collective-permute-done.9.refs_5_
  178.6 12.1 %shard_map.85 = (f32[512,512]{1,0:T(8,128)}, f32[512,512]{1,0:T(8,128)}, f32[512,512]{1,0:T(8,128)}, f32[512,512]{1,0:T(8,128)}, f32[512,512]{1,0:T(8,128)}, /*index=5*/f32[512,512]{1,0:T(8,128)}, f32[8,256,512]{2,1,0:T(8,128)}) custom-call(f32[512,512]{1,0:T(8,128)} %add_divide_fusion.inv_ref.refs_0_, f32[512,128]{1,0:T(8,128)} %pad.4.wts.refs_1_, ...), custom_call_target="tpu_custom_call" | custom-call | flops 1 | bytes 1 | tf_op jit(solution)/shard_map/pallas_call | solution.py:229
  190.7 0.0 collective-permute-done.4.refs_5_
  190.7 0.0 copy-start.7
  190.7 1.9 collective-permute-start.13
  192.6 2.6 %collective-permute-start.12 = (f32[512,512]{1,0:T(8,128)}, f32[512,512]{1,0:T(8,128)S(1)}, u32[]{:S(2)}, u32[]{:S(2)}) collective-permute-start(f32[512,512]{1,0:T(8,128)} %get-tuple-element.60), channel_id=1, source_target_pairs={{2,0},{4,2},{6,4},{8,6},{10,8},{12,10},{14,12},{18,16},{20,18},{22... | collective-permute-start | bytes 3145736 | tf_op jit(solution)/shard_map/ppermute | solution.py:387
  195.2 5.1 %collective-permute-done.10.refs_4_ = f32[1,256,512]{2,1,0:T(8,128)} collective-permute-done((f32[1,256,512]{2,1,0:T(8,128)}, f32[1,256,512]{2,1,0:T(8,128)}, u32[]{:S(2)}, u32[]{:S(2)}) %collective-permute-start.10) | collective-permute-done | bytes 524320 | tf_op jit(solution)/shard_map/ppermute | solution.py:371
  200.3 0.0 collective-permute-start.11
  200.4 1.5 collective-permute-start.5
  201.8 1.8 collective-permute-done.7.refs_5_
  203.6 9.3 %shard_map.86 = (f32[512,512]{1,0:T(8,128)}, f32[512,512]{1,0:T(8,128)}, f32[8,256,512]{2,1,0:T(8,128)}) custom-call(f32[512,512]{1,0:T(8,128)} %add_divide_fusion.inv_ref.refs_0_, f32[512,128]{1,0:T(8,128)} %pad.4.wts.refs_1_, bf16[512,512]{1,0:T(8,128)(2,1)} %get-tuple-element.71.refs_0_.refs_2_.refs_3_, ...), custom_call_target="tpu_custom_call", output_to_operand_aliasing={{2}: (13, {})} | custom-call | flops 1 | bytes 1 | tf_op jit(solution)/shard_map/pallas_call | solution.py:261
  212.9 1.4 collective-permute-done.11.refs_5_
  214.3 6.2 %shard_map.87 = (f32[512,512]{1,0:T(8,128)}, f32[8,256,512]{2,1,0:T(8,128)}) custom-call(f32[512,512]{1,0:T(8,128)} %add_divide_fusion.inv_ref.refs_0_, f32[512,128]{1,0:T(8,128)} %pad.4.wts.refs_1_, bf16[512,512]{1,0:T(8,128)(2,1)} %get-tuple-element.71.refs_0_.refs_2_.refs_3_, ...), custom_call_target="tpu_custom_call", output_to_operand_aliasing={{1}: (13, {})} | custom-call | flops 1 | bytes 1 | tf_op jit(solution)/shard_map/pallas_call | solution.py:315
  220.5 0.0 collective-permute-done.13.edge_ref
  220.6 1.0 copy-done.6
  221.5 5.2 %shard_map.88.refs_15_ = f32[8,256,512]{2,1,0:T(8,128)} custom-call(f32[512,512]{1,0:T(8,128)} %add_divide_fusion.inv_ref.refs_0_, f32[512,128]{1,0:T(8,128)} %pad.4.wts.refs_1_, f32[8,512,512]{2,1,0:T(8,128)} %get-tuple-element.37.refs_8_.refs_6_.part.refs_2_, f32[512,512]{1,0:T(8,128)} %get-tuple-element.61.mid_ref, ...), custom_call_target="tpu_custom_call", output_to_operand_aliasing={{}: (10, {})} | custom-call | flops 1 | bytes 1 | tf_op jit(solution)/shard_map/pallas_call | solution.py:283
  226.8 0.0 collective-permute-done.5.refs_6_
  226.8 0.0 collective-permute-done.12.refs_10_
  226.8 1.0 copy-done.5
  227.8 9.7 %shard_map.89 = f32[8,256,512]{2,1,0:T(8,128)} custom-call(f32[512,512]{1,0:T(8,128)} %add_divide_fusion.inv_ref.refs_0_, f32[512,128]{1,0:T(8,128)} %pad.4.wts.refs_1_, f32[8,512,512]{2,1,0:T(8,128)} %get-tuple-element.37.refs_8_.refs_6_.part.refs_2_, bf16[512,512]{1,0:T(8,128)(2,1)} %get-tuple-element.71.refs_0_.refs_2_.refs_3_, ...), custom_call_target="tpu_custom_call", output_to_operand_aliasing={{}: (15, {})} | custom-call | flops 1 | bytes 1 | tf_op jit(solution)/shard_map/pallas_call | solution.py:355
  (15 shorter events, 0.1 us)
Async XLA Ops:
  3.6 13.4 %copy-start = (f32[2,256,512]{2,1,0:T(8,128)S(1)}, f32[2,256,512]{2,1,0:T(8,128)}, u32[]{:S(2)}) copy-start(f32[2,256,512]{2,1,0:T(8,128)} %shard_map.82.refs_2_) | copy-start | bytes 3145732
  3.6 16.6 %copy-start.1 = (bf16[512,512]{1,0:T(8,128)(2,1)S(1)}, bf16[512,512]{1,0:T(8,128)(2,1)}, u32[]{:S(2)}) copy-start(bf16[512,512]{1,0:T(8,128)(2,1)} %constant.44.clone.high) | copy-start | bytes 1572868
  3.6 16.6 %copy-start.2 = (bf16[512,512]{1,0:T(8,128)(2,1)S(1)}, bf16[512,512]{1,0:T(8,128)(2,1)}, u32[]{:S(2)}) copy-start(bf16[512,512]{1,0:T(8,128)(2,1)} %constant.45.clone.low) | copy-start | bytes 1572868
  3.6 106.0 %copy-start.8 = (f32[2,512]{1,0:T(2,128)S(1)}, f32[2,512]{1,0:T(2,128)}, u32[]{:S(2)}) copy-start(f32[2,512]{1,0:T(2,128)} %param.11) | copy-start | bytes 12292
  12.7 118.7 %collective-permute-start.1 = (f32[6,256,512]{2,1,0:T(8,128)}, f32[6,256,512]{2,1,0:T(8,128)}, u32[]{:S(2)}, u32[]{:S(2)}) collective-permute-start(f32[6,256,512]{2,1,0:T(8,128)} %get-tuple-element.36.refs_4_), channel_id=1, source_target_pairs={{0,1},{1,0},{2,3},{3,2},{4,5},{5,4},{6,7},{7,6},{8,9},{9,8},{10,11... | collective-permute-start | bytes 9437192 | tf_op jit(solution)/shard_map/ppermute | solution.py:379
  13.9 94.8 %collective-permute-start.2 = (f32[2,256,512]{2,1,0:T(8,128)}, f32[2,256,512]{2,1,0:T(8,128)}, u32[]{:S(2)}, u32[]{:S(2)}) collective-permute-start(f32[2,256,512]{2,1,0:T(8,128)} %get-tuple-element.39), channel_id=1, source_target_pairs={{0,30},{2,28},{4,26},{6,24},{8,22},{10,20},{12,18},{14,16},{16,14}... | collective-permute-start | bytes 3145736 | tf_op jit(solution)/shard_map/ppermute | solution.py:371
  17.0 114.1 %collective-permute-start.8 = (f32[2,256,512]{2,1,0:T(8,128)S(1)}, f32[2,256,512]{2,1,0:T(8,128)}, u32[]{:S(2)}, u32[]{:S(2)}) collective-permute-start(f32[2,256,512]{2,1,0:T(8,128)S(1)} %copy-done), channel_id=1, source_target_pairs={{0,30},{2,28},{4,26},{6,24},{8,22},{10,20},{12,18},{14,16},{16,14}... | collective-permute-start | bytes 3145736 | tf_op jit(solution)/shard_map/ppermute | solution.py:371
  17.0 114.3 %collective-permute-start = (f32[2,256,512]{2,1,0:T(8,128)S(1)}, f32[2,256,512]{2,1,0:T(8,128)}, u32[]{:S(2)}, u32[]{:S(2)}) collective-permute-start(f32[2,256,512]{2,1,0:T(8,128)S(1)} %copy-done), channel_id=1, source_target_pairs={{0,1},{1,0},{2,3},{3,2},{4,5},{5,4},{6,7},{7,6},{8,9},{9,8},{10,11... | collective-permute-start | bytes 3145736 | tf_op jit(solution)/shard_map/ppermute | solution.py:379
  17.3 158.8 %collective-permute-start.6 = (f32[2,256,512]{2,1,0:T(8,128)}, f32[2,256,512]{2,1,0:T(8,128)S(1)}, u32[]{:S(2)}, u32[]{:S(2)}) collective-permute-start(f32[2,256,512]{2,1,0:T(8,128)} %get-tuple-element.41), channel_id=1, source_target_pairs={{0,30},{2,28},{4,26},{6,24},{8,22},{10,20},{12,18},{14,16},{16,14}... | collective-permute-start | bytes 3145736 | tf_op jit(solution)/shard_map/ppermute | solution.py:371
  108.7 39.6 %collective-permute-start.3 = (f32[2,256,512]{2,1,0:T(8,128)}, f32[2,256,512]{2,1,0:T(8,128)S(1)}, u32[]{:S(2)}, u32[]{:S(2)}) collective-permute-start(f32[2,256,512]{2,1,0:T(8,128)} %collective-permute-done.2.refs_6_), channel_id=1, source_target_pairs={{0,1},{1,0},{2,3},{3,2},{4,5},{5,4},{6,7},{7,6},{8,9},{9,8},{10,11... | collective-permute-start | bytes 3145736 | tf_op jit(solution)/shard_map/ppermute | solution.py:379
  131.1 47.5 %collective-permute-start.9 = (f32[2,256,512]{2,1,0:T(8,128)}, f32[2,256,512]{2,1,0:T(8,128)}, u32[]{:S(2)}, u32[]{:S(2)}) collective-permute-start(f32[2,256,512]{2,1,0:T(8,128)} %collective-permute-done.8.refs_4_), channel_id=1, source_target_pairs={{0,1},{1,0},{2,3},{3,2},{4,5},{5,4},{6,7},{7,6},{8,9},{9,8},{10,11... | collective-permute-start | bytes 3145736 | tf_op jit(solution)/shard_map/ppermute | solution.py:379
  148.3 30.3 %copy-start.4 = (f32[2,256,512]{2,1,0:T(8,128)}, f32[2,256,512]{2,1,0:T(8,128)S(1)}, u32[]{:S(2)}) copy-start(f32[2,256,512]{2,1,0:T(8,128)S(1)} %collective-permute-done.3.refs_7_) | copy-start | bytes 3145732
  148.3 42.3 %collective-permute-start.4 = (f32[1,256,512]{2,1,0:T(8,128)}, f32[1,256,512]{2,1,0:T(8,128)S(1)}, u32[]{:S(2)}, u32[]{:S(2)}) collective-permute-start(f32[1,256,512]{2,1,0:T(8,128)} %get-tuple-element.40), channel_id=1, source_target_pairs={{0,30},{2,28},{4,26},{6,24},{8,22},{10,20},{12,18},{14,16},{16,14}... | collective-permute-start | bytes 1572872 | tf_op jit(solution)/shard_map/ppermute | solution.py:371
  176.0 14.7 %copy-start.3 = (f32[2,256,512]{2,1,0:T(8,128)}, f32[2,256,512]{2,1,0:T(8,128)S(1)}, u32[]{:S(2)}) copy-start(f32[2,256,512]{2,1,0:T(8,128)S(1)} %collective-permute-done.6.refs_4_) | copy-start | bytes 3145732
  176.0 24.3 %collective-permute-start.10 = (f32[1,256,512]{2,1,0:T(8,128)}, f32[1,256,512]{2,1,0:T(8,128)}, u32[]{:S(2)}, u32[]{:S(2)}) collective-permute-start(f32[1,256,512]{2,1,0:T(8,128)} %get-tuple-element.52), channel_id=1, source_target_pairs={{0,30},{2,28},{4,26},{6,24},{8,22},{10,20},{12,18},{14,16},{16,14}... | collective-permute-start | bytes 1572872 | tf_op jit(solution)/shard_map/ppermute | solution.py:371
  178.4 25.3 %collective-permute-start.7 = (f32[2,256,512]{2,1,0:T(8,128)S(1)}, f32[2,256,512]{2,1,0:T(8,128)}, u32[]{:S(2)}, u32[]{:S(2)}) collective-permute-start(f32[2,256,512]{2,1,0:T(8,128)S(1)} %collective-permute-done.6.refs_4_), channel_id=1, source_target_pairs={{0,1},{1,0},{2,3},{3,2},{4,5},{5,4},{6,7},{7,6},{8,9},{9,8},{10,11... | collective-permute-start | bytes 3145736 | tf_op jit(solution)/shard_map/ppermute | solution.py:379
  190.7 29.8 %copy-start.7 = (f32[1,256,512]{2,1,0:T(8,128)}, f32[1,256,512]{2,1,0:T(8,128)S(1)}, u32[]{:S(2)}) copy-start(f32[1,256,512]{2,1,0:T(8,128)S(1)} %collective-permute-done.4.refs_5_) | copy-start | bytes 1572868
  190.7 29.8 %collective-permute-start.13 = (f32[512,512]{1,0:T(8,128)}, f32[512,512]{1,0:T(8,128)S(1)}, u32[]{:S(2)}, u32[]{:S(2)}) collective-permute-start(f32[512,512]{1,0:T(8,128)} %get-tuple-element.63), channel_id=1, source_target_pairs={{0,2},{2,4},{4,6},{6,8},{8,10},{10,12},{12,14},{16,18},{18,20},{20... | collective-permute-start | bytes 3145736 | tf_op jit(solution)/shard_map/ppermute | solution.py:386
  192.6 34.1 %collective-permute-start.12 = (f32[512,512]{1,0:T(8,128)}, f32[512,512]{1,0:T(8,128)S(1)}, u32[]{:S(2)}, u32[]{:S(2)}) collective-permute-start(f32[512,512]{1,0:T(8,128)} %get-tuple-element.60), channel_id=1, source_target_pairs={{2,0},{4,2},{6,4},{8,6},{10,8},{12,10},{14,12},{18,16},{20,18},{22... | collective-permute-start | bytes 3145736 | tf_op jit(solution)/shard_map/ppermute | solution.py:387
  200.3 14.0 %collective-permute-start.11 = (f32[1,256,512]{2,1,0:T(8,128)}, f32[1,256,512]{2,1,0:T(8,128)}, u32[]{:S(2)}, u32[]{:S(2)}) collective-permute-start(f32[1,256,512]{2,1,0:T(8,128)} %collective-permute-done.10.refs_4_), channel_id=1, source_target_pairs={{0,1},{1,0},{2,3},{3,2},{4,5},{5,4},{6,7},{7,6},{8,9},{9,8},{10,11... | collective-permute-start | bytes 1572872 | tf_op jit(solution)/shard_map/ppermute | solution.py:379
  200.4 26.4 %collective-permute-start.5 = (f32[1,256,512]{2,1,0:T(8,128)S(1)}, f32[1,256,512]{2,1,0:T(8,128)}, u32[]{:S(2)}, u32[]{:S(2)}) collective-permute-start(f32[1,256,512]{2,1,0:T(8,128)S(1)} %collective-permute-done.4.refs_5_), channel_id=1, source_target_pairs={{0,1},{1,0},{2,3},{3,2},{4,5},{5,4},{6,7},{7,6},{8,9},{9,8},{10,11... | collective-permute-start | bytes 1572872 | tf_op jit(solution)/shard_map/ppermute | solution.py:379
  220.5 1.0 copy-start.6
  226.8 1.0 copy-start.5

commit v3 on v2

--- a/solution.py
+++ b/solution.py
@@ -89,37 +89,46 @@
 
 def row_modes(source, labels, voltages, planes, uses):
     rows = source.shape[1]
-    first, stride = planes[0], planes[1] - planes[0]
-    count = len(planes)
-
-    def body(volts, source_ref, labels_ref, high, low, *outs):
-        label = labels_ref[...]
-        pick = jnp.full(label.shape, volts[0], F32)
-        for region in range(1, volts.shape[0]):
-            pick = jnp.where(label == region, volts[region], pick)
-        modes = dot3(split(source_ref[...] + pick), (high[...], low[...]))
+    steps = len(planes) // 2
+
+    def body(volts, *refs):
+        high, low = refs[4:6]
+        charge = []
+        for source_ref, labels_ref in (refs[0:2], refs[2:4]):
+            label = labels_ref[...]
+            pick = jnp.full(label.shape, volts[0], F32)
+            for region in range(1, volts.shape[0]):
+                pick = jnp.where(label == region, volts[region], pick)
+            charge.append(source_ref[...] + pick)
+        modes = dot3(split(jnp.concatenate(charge, axis=0)), (high[...], low[...]))
+        modes = modes.reshape(2, rows, NY)
         g = pl.program_id(0)
-        for use, out in zip(uses, outs):
+        for use, out in zip(uses, refs[6:]):
             start = planes.index(use[0])
-            if len(use) == count:
+            if len(use) == len(planes):
                 out[...] = modes
             else:
-                pl.when((g >= start) & (g < start + len(use)))(functools.partial(put, out, modes))
-
-    block = pl.BlockSpec((None, rows, NY), lambda g: (first + stride * g, 0, 0))
+                part = modes if len(use) == 2 else modes[start % 2:start % 2 + 1]
+                pl.when(g == start // 2)(functools.partial(put, out, part))
+
+    def block(which):
+        if steps == 1:
+            return pl.BlockSpec((None, rows, NY), lambda g: (planes[which], 0, 0))
+        return pl.BlockSpec((None, rows, NY), lambda g: (planes[which] - 2 * g, 0, 0))
 
     def slot(use):
-        start, last = planes.index(use[0]), len(use) - 1
-        return pl.BlockSpec((None, rows, NY), lambda g: (jnp.clip(g - start, 0, last), 0, 0))
-
-    return call(
-        body,
-        count,
-        [pl.BlockSpec(memory_space=pltpu.SMEM), block, block, whole((NY, NY)), whole((NY, NY))],
+        if len(use) == len(planes):
+            return pl.BlockSpec((2, rows, NY), lambda g: (g, 0, 0))
+        return pl.BlockSpec((len(use), rows, NY), lambda g: (0, 0, 0))
+
+    return call(
+        body,
+        steps,
+        [pl.BlockSpec(memory_space=pltpu.SMEM)] + [block(0)] * 2 + [block(1)] * 2 + [whole((NY, NY))] * 2,
         [slot(use) for use in uses],
         [jax.ShapeDtypeStruct((len(use), rows, NY), F32) for use in uses],
         COST["rows"],
-    )(voltages, source, labels, *[jnp.asarray(part) for part in BASIS_T])
+    )(voltages, source, labels, source, labels, *[jnp.asarray(part) for part in BASIS_T])
 
 
 def put(out, value):
@@ -433,7 +442,7 @@
     passed = [gather_rows(after(sent[0], *x_table, *rows_table, inverse, weights, flags))]
     partial, own_first, own_last = own_part(flags, inverse, weights, x_table, ends, others)
     passed.append(gather_rows(sent[1]))
-    sent += [to_mirror(after(block, passed[1][-1], partial)) for block in rest[2:]]
+    sent += [to_mirror(after(block, passed[0][-1], partial)) for block in rest[2:]]
     passed.append(gather_rows(after(sent[2], partial)))
     top, plane_0, low, mid, to_above, to_below, out = first_planes(
         inverse, weights, x_table, [after(passed[0][0], sent[2])] + passed[0][1:], passed[1],

time: 239 us -> 237 us (level)
  no operation moved by 1% of the time
where the time goes in v3:
time: 237 us; the launch traced here: 236 us
  waiting for transfers between devices  137 us (58%)
  Pallas kernels  71.6 us (30%)
  starting transfers between devices  19.4 us (8%)
  local copies, waits for them, and re-layouts  5.95 us (3%)
    ppermute x5, waiting for transfers between devices, to_mirror(): lax.ppermute(block, 'axial', [(i, count - 1 - i) for i in range(count)])  135 us
    pallas_call x1, Pallas kernels, own_part(): call(body, total + 1, [pl.BlockSpec(memory_space=pltpu.SMEM), whole((NX,...  16.9 us
    pallas_call x2, Pallas kernels, row_modes(): call(body, steps, [pl.BlockSpec(memory_space=pltpu.SMEM)] + [block(0)] *...  12.3 us
    pallas_call x1, Pallas kernels, first_planes(): call(body, 4, [whole((NX, NY)), whole((NX, 128))] + [whole((NX, NX))] * 2...  12.1 us
    ppermute x5, starting transfers between devices, to_mirror(): lax.ppermute(block, 'axial', [(i, count - 1 - i) for i in range(count)])  11 us
    pallas_call x1, Pallas kernels, last_planes(): call(body, 3, [whole((NX, NY)), whole((NX, 128)), pl.BlockSpec((None, NX,...  9.67 us
    pallas_call x1, Pallas kernels, next_planes(): call(body, 2, [whole((NX, NY)), whole((NX, 128))] + [whole((NX, NX))] * 2...  9.27 us
    pallas_call x1, Pallas kernels, step(): call(body, 1, [whole((NX, NY)), whole((NX, 128))] + [whole((NX, NX))] * 2...  6.21 us
  transfers between devices with their start and end apart: 14, of which 6 were waited for; matrix products, arithmetic and copies ran while one was open for 3% of the time, Pallas kernels for 21%

profile of v3, /device:TPU:9, one launch (start us, length us, event | category | flops | bytes accessed | tf_op | source)
XLA Modules:
  0.0 235.9 jit_solution(2905886154700541046)
XLA Ops:
  0.0 3.9 %shard_map.82.refs_2_ = f32[2,256,512]{2,1,0:T(8,128)} custom-call(f32[4]{0:T(128)} %volts.2, f32[8,256,512]{2,1,0:T(8,128)} %refs_2_.4, s32[8,256,512]{2,1,0:T(8,128)} %refs_3_.4, f32[8,256,512]{2,1,0:T(8,128)} %refs_2_.4, s32[8,256,512]{2,1,0:T(8,128)} %refs_3_.4, bf16[512,512]{1,0:T(8,128)(2,1)} %constant.44.clone.refs_4_, ...), custom_call_target="tpu_custom_call" | custom-call | flops 1 | bytes 1 | tf_op jit(solution)/shard_map/pallas_call | solution.py:124
  3.9 0.0 copy-start.2
  3.9 8.4 %shard_map.83 = (f32[6,256,512]{2,1,0:T(8,128)}, f32[2,256,512]{2,1,0:T(8,128)}, f32[2,256,512]{2,1,0:T(8,128)}, f32[1,256,512]{2,1,0:T(8,128)}, f32[1,256,512]{2,1,0:T(8,128)}) custom-call(f32[4]{0:T(128)} %volts.2, f32[8,256,512]{2,1,0:T(8,128)} %refs_2_.4, s32[8,256,512]{2,1,0:T(8,128)} %refs_3_.4, f32[8,256,512]{2,1,0:T(8,128)} %refs_2_.4, ...), custom_call_target="tpu_custom_call" | custom-call | flops 1 | bytes 1 | tf_op jit(solution)/shard_map/pallas_call | solution.py:124
  12.3 1.3 collective-permute-start.1
  13.6 3.1 %collective-permute-start.2 = (f32[2,256,512]{2,1,0:T(8,128)S(1)}, f32[2,256,512]{2,1,0:T(8,128)S(1)}, u32[]{:S(2)}, u32[]{:S(2)}) collective-permute-start(f32[2,256,512]{2,1,0:T(8,128)S(1)} %copy-done), channel_id=1, source_target_pairs={{0,30},{2,28},{4,26},{6,24},{8,22},{10,20},{12,18},{14,16},{16,14}... | collective-permute-start | bytes 3145736 | tf_op jit(solution)/shard_map/ppermute | solution.py:380
  16.7 0.3 collective-permute-start
  16.9 0.3 collective-permute-start.8
  17.3 0.0 copy-done.8
  17.3 0.7 add_convert_fusion.flag
  18.0 0.1 copy.23
  18.1 0.7 pad.4.wts.refs_1_
  18.9 0.0 copy-done.2
  18.9 0.8 constant_dynamic-slice_fusion
  19.7 2.2 constant_dynamic-slice_fusion.2
  21.9 1.2 add_divide_fusion.inv_ref.refs_0_
  23.2 85.0 %collective-permute-done.2.refs_4_ = f32[2,256,512]{2,1,0:T(8,128)S(1)} collective-permute-done((f32[2,256,512]{2,1,0:T(8,128)S(1)}, f32[2,256,512]{2,1,0:T(8,128)S(1)}, u32[]{:S(2)}, u32[]{:S(2)}) %collective-permute-start.2) | collective-permute-done | bytes 1048608 | tf_op jit(solution)/shard_map/ppermute | solution.py:380
  108.2 0.3 collective-permute-start.3
  108.5 2.5 %collective-permute-start.6 = (f32[2,256,512]{2,1,0:T(8,128)}, f32[2,256,512]{2,1,0:T(8,128)S(1)}, u32[]{:S(2)}, u32[]{:S(2)}) collective-permute-start(f32[2,256,512]{2,1,0:T(8,128)} %get-tuple-element.41), channel_id=1, source_target_pairs={{0,30},{2,28},{4,26},{6,24},{8,22},{10,20},{12,18},{14,16},{16,14}... | collective-permute-start | bytes 3145736 | tf_op jit(solution)/shard_map/ppermute | solution.py:380
  111.0 19.6 %collective-permute-done.8.refs_6_ = f32[2,256,512]{2,1,0:T(8,128)} collective-permute-done((f32[2,256,512]{2,1,0:T(8,128)}, f32[2,256,512]{2,1,0:T(8,128)}, u32[]{:S(2)}, u32[]{:S(2)}) %collective-permute-start.8) | collective-permute-done | bytes 1048608 | tf_op jit(solution)/shard_map/ppermute | solution.py:380
  130.5 0.3 collective-permute-start.9
  130.8 0.0 collective-permute-done.refs_3_
  130.8 0.0 collective-permute-done.1.refs_5_
  130.8 16.9 %shard_map.84 = (f32[8,512,512]{2,1,0:T(8,128)}, f32[512,512]{1,0:T(8,128)}, f32[512,512]{1,0:T(8,128)}) custom-call(f32[2]{0:T(128)} %add_convert_fusion.flag, f32[512,512]{1,0:T(8,128)} %add_divide_fusion.inv_ref.refs_0_, f32[512,128]{1,0:T(8,128)} %pad.4.wts.refs_1_, bf16[512,512]{1,0:T(8,128)(2,1)} %get-tuple-element.71.refs_0_.refs_2_.refs_3_, ...), custom_call_target="tpu_custom_call" | custom-call | flops 1 | bytes 1 | tf_op jit(solution)/shard_map/pallas_call | solution.py:177
  147.8 0.0 collective-permute-done.3.refs_5_
  147.8 2.8 %collective-permute-start.4 = (f32[1,256,512]{2,1,0:T(8,128)}, f32[1,256,512]{2,1,0:T(8,128)S(1)}, u32[]{:S(2)}, u32[]{:S(2)}) collective-permute-start(f32[1,256,512]{2,1,0:T(8,128)} %get-tuple-element.40), channel_id=1, source_target_pairs={{0,30},{2,28},{4,26},{6,24},{8,22},{10,20},{12,18},{14,16},{16,14}... | collective-permute-start | bytes 1572872 | tf_op jit(solution)/shard_map/ppermute | solution.py:380
  150.6 24.9 %collective-permute-done.6.refs_4_ = f32[2,256,512]{2,1,0:T(8,128)S(1)} collective-permute-done((f32[2,256,512]{2,1,0:T(8,128)}, f32[2,256,512]{2,1,0:T(8,128)S(1)}, u32[]{:S(2)}, u32[]{:S(2)}) %collective-permute-start.6) | collective-permute-done | bytes 1048608 | tf_op jit(solution)/shard_map/ppermute | solution.py:380
  175.5 2.4 collective-permute-start.10
  177.8 0.3 collective-permute-start.7
  178.1 0.0 collective-permute-done.9.refs_7_
  178.1 12.1 %shard_map.85 = (f32[512,512]{1,0:T(8,128)}, f32[512,512]{1,0:T(8,128)}, f32[512,512]{1,0:T(8,128)}, f32[512,512]{1,0:T(8,128)}, f32[512,512]{1,0:T(8,128)}, /*index=5*/f32[512,512]{1,0:T(8,128)}, f32[8,256,512]{2,1,0:T(8,128)}) custom-call(f32[512,512]{1,0:T(8,128)} %add_divide_fusion.inv_ref.refs_0_, f32[512,128]{1,0:T(8,128)} %pad.4.wts.refs_1_, ...), custom_call_target="tpu_custom_call" | custom-call | flops 1 | bytes 1 | tf_op jit(solution)/shard_map/pallas_call | solution.py:238
  190.2 0.0 collective-permute-done.4.refs_5_
  190.2 1.9 collective-permute-start.13
  192.1 2.6 %collective-permute-start.12 = (f32[512,512]{1,0:T(8,128)}, f32[512,512]{1,0:T(8,128)S(1)}, u32[]{:S(2)}, u32[]{:S(2)}) collective-permute-start(f32[512,512]{1,0:T(8,128)} %get-tuple-element.60), channel_id=1, source_target_pairs={{2,0},{4,2},{6,4},{8,6},{10,8},{12,10},{14,12},{18,16},{20,18},{22... | collective-permute-start | bytes 3145736 | tf_op jit(solution)/shard_map/ppermute | solution.py:396
  194.7 5.1 %collective-permute-done.10.refs_4_ = f32[1,256,512]{2,1,0:T(8,128)} collective-permute-done((f32[1,256,512]{2,1,0:T(8,128)}, f32[1,256,512]{2,1,0:T(8,128)}, u32[]{:S(2)}, u32[]{:S(2)}) %collective-permute-start.10) | collective-permute-done | bytes 524320 | tf_op jit(solution)/shard_map/ppermute | solution.py:380
  199.8 0.0 collective-permute-start.11
  199.8 1.5 collective-permute-start.5
  201.3 1.8 collective-permute-done.7.refs_5_
  203.0 1.0 copy-done.6
  204.0 9.3 %shard_map.86 = (f32[512,512]{1,0:T(8,128)}, f32[512,512]{1,0:T(8,128)}, f32[8,256,512]{2,1,0:T(8,128)}) custom-call(f32[512,512]{1,0:T(8,128)} %add_divide_fusion.inv_ref.refs_0_, f32[512,128]{1,0:T(8,128)} %pad.4.wts.refs_1_, bf16[512,512]{1,0:T(8,128)(2,1)} %get-tuple-element.71.refs_0_.refs_2_.refs_3_, ...), custom_call_target="tpu_custom_call", output_to_operand_aliasing={{2}: (13, {})} | custom-call | flops 1 | bytes 1 | tf_op jit(solution)/shard_map/pallas_call | solution.py:270
  213.3 0.5 collective-permute-done.11.refs_5_
  213.8 6.2 %shard_map.87 = (f32[512,512]{1,0:T(8,128)}, f32[8,256,512]{2,1,0:T(8,128)}) custom-call(f32[512,512]{1,0:T(8,128)} %add_divide_fusion.inv_ref.refs_0_, f32[512,128]{1,0:T(8,128)} %pad.4.wts.refs_1_, bf16[512,512]{1,0:T(8,128)(2,1)} %get-tuple-element.71.refs_0_.refs_2_.refs_3_, ...), custom_call_target="tpu_custom_call", output_to_operand_aliasing={{1}: (13, {})} | custom-call | flops 1 | bytes 1 | tf_op jit(solution)/shard_map/pallas_call | solution.py:324
  220.0 0.0 copy-done.7
  220.0 0.0 collective-permute-done.13.edge_ref
  220.0 5.2 %shard_map.88.refs_15_ = f32[8,256,512]{2,1,0:T(8,128)} custom-call(f32[512,512]{1,0:T(8,128)} %add_divide_fusion.inv_ref.refs_0_, f32[512,128]{1,0:T(8,128)} %pad.4.wts.refs_1_, f32[8,512,512]{2,1,0:T(8,128)} %get-tuple-element.37.refs_8_.refs_6_.part.refs_2_, f32[512,512]{1,0:T(8,128)} %get-tuple-element.61.mid_ref, ...), custom_call_target="tpu_custom_call", output_to_operand_aliasing={{}: (10, {})} | custom-call | flops 1 | bytes 1 | tf_op jit(solution)/shard_map/pallas_call | solution.py:292
  225.2 0.0 collective-permute-done.5.refs_6_
  225.2 0.0 collective-permute-done.12.refs_10_
  225.3 1.0 copy-done.5
  226.2 9.7 %shard_map.89 = f32[8,256,512]{2,1,0:T(8,128)} custom-call(f32[512,512]{1,0:T(8,128)} %add_divide_fusion.inv_ref.refs_0_, f32[512,128]{1,0:T(8,128)} %pad.4.wts.refs_1_, f32[8,512,512]{2,1,0:T(8,128)} %get-tuple-element.37.refs_8_.refs_6_.part.refs_2_, bf16[512,512]{1,0:T(8,128)(2,1)} %get-tuple-element.71.refs_0_.refs_2_.refs_3_, ...), custom_call_target="tpu_custom_call", output_to_operand_aliasing={{}: (15, {})} | custom-call | flops 1 | bytes 1 | tf_op jit(solution)/shard_map/pallas_call | solution.py:364
  (15 shorter events, 0.1 us)
Async XLA Ops:
  3.9 9.7 %copy-start = (f32[2,256,512]{2,1,0:T(8,128)S(1)}, f32[2,256,512]{2,1,0:T(8,128)}, u32[]{:S(2)}) copy-start(f32[2,256,512]{2,1,0:T(8,128)} %shard_map.82.refs_2_) | copy-start | bytes 3145732
  3.9 13.4 %copy-start.8 = (f32[2,512]{1,0:T(2,128)S(1)}, f32[2,512]{1,0:T(2,128)}, u32[]{:S(2)}) copy-start(f32[2,512]{1,0:T(2,128)} %param.11) | copy-start | bytes 12292
  3.9 15.0 %copy-start.1 = (bf16[512,512]{1,0:T(8,128)(2,1)S(1)}, bf16[512,512]{1,0:T(8,128)(2,1)}, u32[]{:S(2)}) copy-start(bf16[512,512]{1,0:T(8,128)(2,1)} %constant.44.clone.refs_4_) | copy-start | bytes 1572868
  3.9 15.0 %copy-start.2 = (bf16[512,512]{1,0:T(8,128)(2,1)S(1)}, bf16[512,512]{1,0:T(8,128)(2,1)}, u32[]{:S(2)}) copy-start(bf16[512,512]{1,0:T(8,128)(2,1)} %constant.45.clone.refs_5_) | copy-start | bytes 1572868
  12.3 118.5 %collective-permute-start.1 = (f32[6,256,512]{2,1,0:T(8,128)}, f32[6,256,512]{2,1,0:T(8,128)}, u32[]{:S(2)}, u32[]{:S(2)}) collective-permute-start(f32[6,256,512]{2,1,0:T(8,128)} %get-tuple-element.36.refs_4_), channel_id=1, source_target_pairs={{0,1},{1,0},{2,3},{3,2},{4,5},{5,4},{6,7},{7,6},{8,9},{9,8},{10,11... | collective-permute-start | bytes 9437192 | tf_op jit(solution)/shard_map/ppermute | solution.py:388
  13.6 94.6 %collective-permute-start.2 = (f32[2,256,512]{2,1,0:T(8,128)S(1)}, f32[2,256,512]{2,1,0:T(8,128)S(1)}, u32[]{:S(2)}, u32[]{:S(2)}) collective-permute-start(f32[2,256,512]{2,1,0:T(8,128)S(1)} %copy-done), channel_id=1, source_target_pairs={{0,30},{2,28},{4,26},{6,24},{8,22},{10,20},{12,18},{14,16},{16,14}... | collective-permute-start | bytes 3145736 | tf_op jit(solution)/shard_map/ppermute | solution.py:380
  16.7 114.2 %collective-permute-start = (f32[2,256,512]{2,1,0:T(8,128)S(1)}, f32[2,256,512]{2,1,0:T(8,128)}, u32[]{:S(2)}, u32[]{:S(2)}) collective-permute-start(f32[2,256,512]{2,1,0:T(8,128)S(1)} %copy-done), channel_id=1, source_target_pairs={{0,1},{1,0},{2,3},{3,2},{4,5},{5,4},{6,7},{7,6},{8,9},{9,8},{10,11... | collective-permute-start | bytes 3145736 | tf_op jit(solution)/shard_map/ppermute | solution.py:388
  16.9 113.6 %collective-permute-start.8 = (f32[2,256,512]{2,1,0:T(8,128)}, f32[2,256,512]{2,1,0:T(8,128)}, u32[]{:S(2)}, u32[]{:S(2)}) collective-permute-start(f32[2,256,512]{2,1,0:T(8,128)} %get-tuple-element.44), channel_id=1, source_target_pairs={{0,30},{2,28},{4,26},{6,24},{8,22},{10,20},{12,18},{14,16},{16,14}... | collective-permute-start | bytes 3145736 | tf_op jit(solution)/shard_map/ppermute | solution.py:380
  108.2 39.6 %copy-start.3 = (f32[2,256,512]{2,1,0:T(8,128)}, f32[2,256,512]{2,1,0:T(8,128)S(1)}, u32[]{:S(2)}) copy-start(f32[2,256,512]{2,1,0:T(8,128)S(1)} %collective-permute-done.2.refs_4_) | copy-start | bytes 3145732
  108.2 39.6 %collective-permute-start.3 = (f32[2,256,512]{2,1,0:T(8,128)S(1)}, f32[2,256,512]{2,1,0:T(8,128)}, u32[]{:S(2)}, u32[]{:S(2)}) collective-permute-start(f32[2,256,512]{2,1,0:T(8,128)S(1)} %collective-permute-done.2.refs_4_), channel_id=1, source_target_pairs={{0,1},{1,0},{2,3},{3,2},{4,5},{5,4},{6,7},{7,6},{8,9},{9,8},{10,11... | collective-permute-start | bytes 3145736 | tf_op jit(solution)/shard_map/ppermute | solution.py:388
  108.5 67.0 %collective-permute-start.6 = (f32[2,256,512]{2,1,0:T(8,128)}, f32[2,256,512]{2,1,0:T(8,128)S(1)}, u32[]{:S(2)}, u32[]{:S(2)}) collective-permute-start(f32[2,256,512]{2,1,0:T(8,128)} %get-tuple-element.41), channel_id=1, source_target_pairs={{0,30},{2,28},{4,26},{6,24},{8,22},{10,20},{12,18},{14,16},{16,14}... | collective-permute-start | bytes 3145736 | tf_op jit(solution)/shard_map/ppermute | solution.py:380
  130.5 47.6 %collective-permute-start.9 = (f32[2,256,512]{2,1,0:T(8,128)}, f32[2,256,512]{2,1,0:T(8,128)}, u32[]{:S(2)}, u32[]{:S(2)}) collective-permute-start(f32[2,256,512]{2,1,0:T(8,128)} %collective-permute-done.8.refs_6_), channel_id=1, source_target_pairs={{0,1},{1,0},{2,3},{3,2},{4,5},{5,4},{6,7},{7,6},{8,9},{9,8},{10,11... | collective-permute-start | bytes 3145736 | tf_op jit(solution)/shard_map/ppermute | solution.py:388
  147.8 42.4 %collective-permute-start.4 = (f32[1,256,512]{2,1,0:T(8,128)}, f32[1,256,512]{2,1,0:T(8,128)S(1)}, u32[]{:S(2)}, u32[]{:S(2)}) collective-permute-start(f32[1,256,512]{2,1,0:T(8,128)} %get-tuple-element.40), channel_id=1, source_target_pairs={{0,30},{2,28},{4,26},{6,24},{8,22},{10,20},{12,18},{14,16},{16,14}... | collective-permute-start | bytes 1572872 | tf_op jit(solution)/shard_map/ppermute | solution.py:380
  175.5 14.7 %copy-start.4 = (f32[2,256,512]{2,1,0:T(8,128)}, f32[2,256,512]{2,1,0:T(8,128)S(1)}, u32[]{:S(2)}) copy-start(f32[2,256,512]{2,1,0:T(8,128)S(1)} %collective-permute-done.6.refs_4_) | copy-start | bytes 3145732
  175.5 24.3 %collective-permute-start.10 = (f32[1,256,512]{2,1,0:T(8,128)}, f32[1,256,512]{2,1,0:T(8,128)}, u32[]{:S(2)}, u32[]{:S(2)}) collective-permute-start(f32[1,256,512]{2,1,0:T(8,128)} %get-tuple-element.52), channel_id=1, source_target_pairs={{0,30},{2,28},{4,26},{6,24},{8,22},{10,20},{12,18},{14,16},{16,14}... | collective-permute-start | bytes 1572872 | tf_op jit(solution)/shard_map/ppermute | solution.py:380
  177.8 25.2 %collective-permute-start.7 = (f32[2,256,512]{2,1,0:T(8,128)S(1)}, f32[2,256,512]{2,1,0:T(8,128)S(1)}, u32[]{:S(2)}, u32[]{:S(2)}) collective-permute-start(f32[2,256,512]{2,1,0:T(8,128)S(1)} %collective-permute-done.6.refs_4_), channel_id=1, source_target_pairs={{0,1},{1,0},{2,3},{3,2},{4,5},{5,4},{6,7},{7,6},{8,9},{9,8},{10,11... | collective-permute-start | bytes 3145736 | tf_op jit(solution)/shard_map/ppermute | solution.py:388
  190.2 29.8 %copy-start.7 = (f32[1,256,512]{2,1,0:T(8,128)}, f32[1,256,512]{2,1,0:T(8,128)S(1)}, u32[]{:S(2)}) copy-start(f32[1,256,512]{2,1,0:T(8,128)S(1)} %collective-permute-done.4.refs_5_) | copy-start | bytes 1572868
  190.2 29.8 %collective-permute-start.13 = (f32[512,512]{1,0:T(8,128)}, f32[512,512]{1,0:T(8,128)}, u32[]{:S(2)}, u32[]{:S(2)}) collective-permute-start(f32[512,512]{1,0:T(8,128)} %get-tuple-element.63), channel_id=1, source_target_pairs={{0,2},{2,4},{4,6},{6,8},{8,10},{10,12},{12,14},{16,18},{18,20},{20... | collective-permute-start | bytes 3145736 | tf_op jit(solution)/shard_map/ppermute | solution.py:395
  192.1 33.1 %collective-permute-start.12 = (f32[512,512]{1,0:T(8,128)}, f32[512,512]{1,0:T(8,128)S(1)}, u32[]{:S(2)}, u32[]{:S(2)}) collective-permute-start(f32[512,512]{1,0:T(8,128)} %get-tuple-element.60), channel_id=1, source_target_pairs={{2,0},{4,2},{6,4},{8,6},{10,8},{12,10},{14,12},{18,16},{20,18},{22... | collective-permute-start | bytes 3145736 | tf_op jit(solution)/shard_map/ppermute | solution.py:396
  199.8 14.0 %collective-permute-start.11 = (f32[1,256,512]{2,1,0:T(8,128)}, f32[1,256,512]{2,1,0:T(8,128)}, u32[]{:S(2)}, u32[]{:S(2)}) collective-permute-start(f32[1,256,512]{2,1,0:T(8,128)} %collective-permute-done.10.refs_4_), channel_id=1, source_target_pairs={{0,1},{1,0},{2,3},{3,2},{4,5},{5,4},{6,7},{7,6},{8,9},{9,8},{10,11... | collective-permute-start | bytes 1572872 | tf_op jit(solution)/shard_map/ppermute | solution.py:388
  199.8 25.4 %collective-permute-start.5 = (f32[1,256,512]{2,1,0:T(8,128)S(1)}, f32[1,256,512]{2,1,0:T(8,128)}, u32[]{:S(2)}, u32[]{:S(2)}) collective-permute-start(f32[1,256,512]{2,1,0:T(8,128)S(1)} %collective-permute-done.4.refs_5_), channel_id=1, source_target_pairs={{0,1},{1,0},{2,3},{3,2},{4,5},{5,4},{6,7},{7,6},{8,9},{9,8},{10,11... | collective-permute-start | bytes 1572872 | tf_op jit(solution)/shard_map/ppermute | solution.py:388
  203.0 1.0 copy-start.6
  225.2 1.0 copy-start.5

commit v4 on v3

--- a/solution.py
+++ b/solution.py
@@ -13,7 +13,7 @@
 NY = 512
 F32 = jnp.float32
 BF16 = jnp.bfloat16
-VMEM_LIMIT = 60 * 1024 * 1024
+VMEM_LIMIT = 63 * 1024 * 1024
 
 
 def table_parts():

time: 237 us -> 236 us (level)
  no operation moved by 1% of the time
where the time goes in v4:
time: 236 us
  waiting for transfers between devices  138 us (58%)
  Pallas kernels  71.8 us (30%)
  starting transfers between devices  19.5 us (8%)
  local copies, waits for them, and re-layouts  5.05 us (2%)
    ppermute x5, waiting for transfers between devices, to_mirror(): lax.ppermute(block, 'axial', [(i, count - 1 - i) for i in range(count)])  134 us
    pallas_call x1, Pallas kernels, own_part(): call(body, total + 1, [pl.BlockSpec(memory_space=pltpu.SMEM), whole((NX,...  16.9 us
    pallas_call x2, Pallas kernels, row_modes(): call(body, steps, [pl.BlockSpec(memory_space=pltpu.SMEM)] + [block(0)] *...  12.2 us
    pallas_call x1, Pallas kernels, first_planes(): call(body, 4, [whole((NX, NY)), whole((NX, 128))] + [whole((NX, NX))] * 2...  12.1 us
    ppermute x5, starting transfers between devices, to_mirror(): lax.ppermute(block, 'axial', [(i, count - 1 - i) for i in range(count)])  11.2 us
    pallas_call x1, Pallas kernels, last_planes(): call(body, 3, [whole((NX, NY)), whole((NX, 128)), pl.BlockSpec((None, NX,...  9.72 us
    pallas_call x1, Pallas kernels, next_planes(): call(body, 2, [whole((NX, NY)), whole((NX, 128))] + [whole((NX, NX))] * 2...  9.3 us
    pallas_call x1, Pallas kernels, step(): call(body, 1, [whole((NX, NY)), whole((NX, 128))] + [whole((NX, NX))] * 2...  6.37 us
  transfers between devices with their start and end apart: 14, of which 6 were waited for; matrix products, arithmetic and copies ran while one was open for 3% of the time, Pallas kernels for 21%

profile of v4, /device:TPU:9, one launch (start us, length us, event | category | flops | bytes accessed | tf_op | source)
XLA Modules:
  0.0 235.9 jit_solution(10369612163345934907)
XLA Ops:
  0.0 3.9 %shard_map.82.refs_2_ = f32[2,256,512]{2,1,0:T(8,128)} custom-call(f32[4]{0:T(128)} %volts.2, f32[8,256,512]{2,1,0:T(8,128)} %refs_2_.4, s32[8,256,512]{2,1,0:T(8,128)} %refs_3_.4, f32[8,256,512]{2,1,0:T(8,128)} %refs_2_.4, s32[8,256,512]{2,1,0:T(8,128)} %refs_3_.4, bf16[512,512]{1,0:T(8,128)(2,1)} %constant.44.clone.refs_4_, ...), custom_call_target="tpu_custom_call" | custom-call | flops 1 | bytes 1 | tf_op jit(solution)/shard_map/pallas_call | solution.py:124
  3.9 0.0 copy-start.2
  3.9 0.0 copy-start
  3.9 8.3 %shard_map.83 = (f32[6,256,512]{2,1,0:T(8,128)}, f32[2,256,512]{2,1,0:T(8,128)}, f32[2,256,512]{2,1,0:T(8,128)}, f32[1,256,512]{2,1,0:T(8,128)}, f32[1,256,512]{2,1,0:T(8,128)}) custom-call(f32[4]{0:T(128)} %volts.2, f32[8,256,512]{2,1,0:T(8,128)} %refs_2_.4, s32[8,256,512]{2,1,0:T(8,128)} %refs_3_.4, f32[8,256,512]{2,1,0:T(8,128)} %refs_2_.4, ...), custom_call_target="tpu_custom_call" | custom-call | flops 1 | bytes 1 | tf_op jit(solution)/shard_map/pallas_call | solution.py:124
  12.2 1.3 collective-permute-start.1
  13.5 3.1 %collective-permute-start.2 = (f32[2,256,512]{2,1,0:T(8,128)}, f32[2,256,512]{2,1,0:T(8,128)}, u32[]{:S(2)}, u32[]{:S(2)}) collective-permute-start(f32[2,256,512]{2,1,0:T(8,128)} %shard_map.82.refs_2_), channel_id=1, source_target_pairs={{0,30},{2,28},{4,26},{6,24},{8,22},{10,20},{12,18},{14,16},{16,14}... | collective-permute-start | bytes 3145736 | tf_op jit(solution)/shard_map/ppermute | solution.py:380
  16.6 0.3 collective-permute-start
  16.8 0.3 collective-permute-start.8
  17.2 0.0 copy-done.2
  17.2 0.6 add_convert_fusion.flag
  17.8 0.1 copy.23
  18.0 0.7 pad.4.wts.refs_1_
  18.7 0.0 copy-done
  18.7 1.8 constant_dynamic-slice_fusion
  20.5 2.3 constant_dynamic-slice_fusion.2
  22.8 1.2 add_divide_fusion.inv_ref.refs_0_
  24.1 84.2 %collective-permute-done.2.refs_4_ = f32[2,256,512]{2,1,0:T(8,128)} collective-permute-done((f32[2,256,512]{2,1,0:T(8,128)}, f32[2,256,512]{2,1,0:T(8,128)}, u32[]{:S(2)}, u32[]{:S(2)}) %collective-permute-start.2) | collective-permute-done | bytes 1048608 | tf_op jit(solution)/shard_map/ppermute | solution.py:380
  108.3 0.3 collective-permute-start.3
  108.6 2.6 %collective-permute-start.6 = (f32[2,256,512]{2,1,0:T(8,128)}, f32[2,256,512]{2,1,0:T(8,128)}, u32[]{:S(2)}, u32[]{:S(2)}) collective-permute-start(f32[2,256,512]{2,1,0:T(8,128)} %get-tuple-element.41), channel_id=1, source_target_pairs={{0,30},{2,28},{4,26},{6,24},{8,22},{10,20},{12,18},{14,16},{16,14}... | collective-permute-start | bytes 3145736 | tf_op jit(solution)/shard_map/ppermute | solution.py:380
  111.2 19.6 %collective-permute-done.8.refs_6_ = f32[2,256,512]{2,1,0:T(8,128)} collective-permute-done((f32[2,256,512]{2,1,0:T(8,128)}, f32[2,256,512]{2,1,0:T(8,128)}, u32[]{:S(2)}, u32[]{:S(2)}) %collective-permute-start.8) | collective-permute-done | bytes 1048608 | tf_op jit(solution)/shard_map/ppermute | solution.py:380
  130.8 0.3 collective-permute-start.9
  131.1 0.0 collective-permute-done.refs_3_
  131.1 0.0 collective-permute-done.1.refs_5_
  131.1 16.9 %shard_map.84 = (f32[8,512,512]{2,1,0:T(8,128)}, f32[512,512]{1,0:T(8,128)}, f32[512,512]{1,0:T(8,128)}) custom-call(f32[2]{0:T(128)} %add_convert_fusion.flag, f32[512,512]{1,0:T(8,128)} %add_divide_fusion.inv_ref.refs_0_, f32[512,128]{1,0:T(8,128)} %pad.4.wts.refs_1_, bf16[512,512]{1,0:T(8,128)(2,1)} %get-tuple-element.71.refs_0_.refs_2_.refs_3_, ...), custom_call_target="tpu_custom_call" | custom-call | flops 1 | bytes 1 | tf_op jit(solution)/shard_map/pallas_call | solution.py:177
  148.0 0.0 collective-permute-done.3.refs_5_
  148.0 2.7 %collective-permute-start.4 = (f32[1,256,512]{2,1,0:T(8,128)}, f32[1,256,512]{2,1,0:T(8,128)S(1)}, u32[]{:S(2)}, u32[]{:S(2)}) collective-permute-start(f32[1,256,512]{2,1,0:T(8,128)} %get-tuple-element.40), channel_id=1, source_target_pairs={{0,30},{2,28},{4,26},{6,24},{8,22},{10,20},{12,18},{14,16},{16,14}... | collective-permute-start | bytes 1572872 | tf_op jit(solution)/shard_map/ppermute | solution.py:380
  150.7 24.9 %collective-permute-done.6.refs_4_ = f32[2,256,512]{2,1,0:T(8,128)} collective-permute-done((f32[2,256,512]{2,1,0:T(8,128)}, f32[2,256,512]{2,1,0:T(8,128)}, u32[]{:S(2)}, u32[]{:S(2)}) %collective-permute-start.6) | collective-permute-done | bytes 1048608 | tf_op jit(solution)/shard_map/ppermute | solution.py:380
  175.6 2.5 %collective-permute-start.10 = (f32[1,256,512]{2,1,0:T(8,128)}, f32[1,256,512]{2,1,0:T(8,128)}, u32[]{:S(2)}, u32[]{:S(2)}) collective-permute-start(f32[1,256,512]{2,1,0:T(8,128)} %get-tuple-element.52), channel_id=1, source_target_pairs={{0,30},{2,28},{4,26},{6,24},{8,22},{10,20},{12,18},{14,16},{16,14}... | collective-permute-start | bytes 1572872 | tf_op jit(solution)/shard_map/ppermute | solution.py:380
  178.1 0.3 collective-permute-start.7
  178.3 0.0 collective-permute-done.9.refs_7_
  178.3 12.1 %shard_map.85 = (f32[512,512]{1,0:T(8,128)}, f32[512,512]{1,0:T(8,128)}, f32[512,512]{1,0:T(8,128)}, f32[512,512]{1,0:T(8,128)}, f32[512,512]{1,0:T(8,128)}, /*index=5*/f32[512,512]{1,0:T(8,128)}, f32[8,256,512]{2,1,0:T(8,128)}) custom-call(f32[512,512]{1,0:T(8,128)} %add_divide_fusion.inv_ref.refs_0_, f32[512,128]{1,0:T(8,128)} %pad.4.wts.refs_1_, ...), custom_call_target="tpu_custom_call" | custom-call | flops 1 | bytes 1 | tf_op jit(solution)/shard_map/pallas_call | solution.py:238
  190.4 0.0 collective-permute-done.4.refs_5_
  190.4 0.0 copy-start.1
  190.4 1.9 collective-permute-start.13
  192.4 2.6 %collective-permute-start.12 = (f32[512,512]{1,0:T(8,128)}, f32[512,512]{1,0:T(8,128)}, u32[]{:S(2)}, u32[]{:S(2)}) collective-permute-start(f32[512,512]{1,0:T(8,128)} %get-tuple-element.60), channel_id=1, source_target_pairs={{2,0},{4,2},{6,4},{8,6},{10,8},{12,10},{14,12},{18,16},{20,18},{22... | collective-permute-start | bytes 3145736 | tf_op jit(solution)/shard_map/ppermute | solution.py:396
  195.0 4.9 %collective-permute-done.10.refs_4_ = f32[1,256,512]{2,1,0:T(8,128)} collective-permute-done((f32[1,256,512]{2,1,0:T(8,128)}, f32[1,256,512]{2,1,0:T(8,128)}, u32[]{:S(2)}, u32[]{:S(2)}) %collective-permute-start.10) | collective-permute-done | bytes 524320 | tf_op jit(solution)/shard_map/ppermute | solution.py:380
  199.9 0.0 collective-permute-start.11
  199.9 1.5 collective-permute-start.5
  201.3 2.2 collective-permute-done.7.refs_5_
  203.5 9.3 %shard_map.86 = (f32[512,512]{1,0:T(8,128)}, f32[512,512]{1,0:T(8,128)}, f32[8,256,512]{2,1,0:T(8,128)}) custom-call(f32[512,512]{1,0:T(8,128)} %add_divide_fusion.inv_ref.refs_0_, f32[512,128]{1,0:T(8,128)} %pad.4.wts.refs_1_, bf16[512,512]{1,0:T(8,128)(2,1)} %get-tuple-element.71.refs_0_.refs_2_.refs_3_, ...), custom_call_target="tpu_custom_call", output_to_operand_aliasing={{2}: (13, {})} | custom-call | flops 1 | bytes 1 | tf_op jit(solution)/shard_map/pallas_call | solution.py:270
  212.8 0.0 copy-done.1
  212.8 1.8 collective-permute-done.11.refs_5_
  214.6 6.4 %shard_map.87 = (f32[512,512]{1,0:T(8,128)}, f32[8,256,512]{2,1,0:T(8,128)}) custom-call(f32[512,512]{1,0:T(8,128)} %add_divide_fusion.inv_ref.refs_0_, f32[512,128]{1,0:T(8,128)} %pad.4.wts.refs_1_, bf16[512,512]{1,0:T(8,128)(2,1)} %get-tuple-element.71.refs_0_.refs_2_.refs_3_, ...), custom_call_target="tpu_custom_call", output_to_operand_aliasing={{1}: (13, {})} | custom-call | flops 1 | bytes 1 | tf_op jit(solution)/shard_map/pallas_call | solution.py:324
  221.0 0.0 collective-permute-done.13.edge_ref
  221.0 5.2 %shard_map.88.refs_15_ = f32[8,256,512]{2,1,0:T(8,128)} custom-call(f32[512,512]{1,0:T(8,128)} %add_divide_fusion.inv_ref.refs_0_, f32[512,128]{1,0:T(8,128)} %pad.4.wts.refs_1_, f32[8,512,512]{2,1,0:T(8,128)} %get-tuple-element.37.refs_8_.refs_6_.part.refs_2_, f32[512,512]{1,0:T(8,128)} %get-tuple-element.61.mid_ref, ...), custom_call_target="tpu_custom_call", output_to_operand_aliasing={{}: (10, {})} | custom-call | flops 1 | bytes 1 | tf_op jit(solution)/shard_map/pallas_call | solution.py:292
  226.2 0.0 collective-permute-done.5.refs_6_
  226.2 0.0 collective-permute-done.12.refs_10_
  226.2 9.7 %shard_map.89 = f32[8,256,512]{2,1,0:T(8,128)} custom-call(f32[512,512]{1,0:T(8,128)} %add_divide_fusion.inv_ref.refs_0_, f32[512,128]{1,0:T(8,128)} %pad.4.wts.refs_1_, f32[8,512,512]{2,1,0:T(8,128)} %get-tuple-element.37.refs_8_.refs_6_.part.refs_2_, bf16[512,512]{1,0:T(8,128)(2,1)} %get-tuple-element.71.refs_0_.refs_2_.refs_3_, ...), custom_call_target="tpu_custom_call", output_to_operand_aliasing={{}: (15, {})} | custom-call | flops 1 | bytes 1 | tf_op jit(solution)/shard_map/pallas_call | solution.py:364
  (3 shorter events, 0.1 us)
Async XLA Ops:
  3.9 13.3 %copy-start.2 = (f32[2,512]{1,0:T(2,128)S(1)}, f32[2,512]{1,0:T(2,128)}, u32[]{:S(2)}) copy-start(f32[2,512]{1,0:T(2,128)} %param.11) | copy-start | bytes 12292
  3.9 14.8 %copy-start = (bf16[512,512]{1,0:T(8,128)(2,1)S(1)}, bf16[512,512]{1,0:T(8,128)(2,1)}, u32[]{:S(2)}) copy-start(bf16[512,512]{1,0:T(8,128)(2,1)} %constant.44.clone.refs_4_) | copy-start | bytes 1572868
  12.2 118.9 %collective-permute-start.1 = (f32[6,256,512]{2,1,0:T(8,128)}, f32[6,256,512]{2,1,0:T(8,128)}, u32[]{:S(2)}, u32[]{:S(2)}) collective-permute-start(f32[6,256,512]{2,1,0:T(8,128)} %get-tuple-element.36.refs_4_), channel_id=1, source_target_pairs={{0,1},{1,0},{2,3},{3,2},{4,5},{5,4},{6,7},{7,6},{8,9},{9,8},{10,11... | collective-permute-start | bytes 9437192 | tf_op jit(solution)/shard_map/ppermute | solution.py:388
  13.5 94.8 %collective-permute-start.2 = (f32[2,256,512]{2,1,0:T(8,128)}, f32[2,256,512]{2,1,0:T(8,128)}, u32[]{:S(2)}, u32[]{:S(2)}) collective-permute-start(f32[2,256,512]{2,1,0:T(8,128)} %shard_map.82.refs_2_), channel_id=1, source_target_pairs={{0,30},{2,28},{4,26},{6,24},{8,22},{10,20},{12,18},{14,16},{16,14}... | collective-permute-start | bytes 3145736 | tf_op jit(solution)/shard_map/ppermute | solution.py:380
  16.6 114.5 %collective-permute-start = (f32[2,256,512]{2,1,0:T(8,128)}, f32[2,256,512]{2,1,0:T(8,128)}, u32[]{:S(2)}, u32[]{:S(2)}) collective-permute-start(f32[2,256,512]{2,1,0:T(8,128)} %shard_map.82.refs_2_), channel_id=1, source_target_pairs={{0,1},{1,0},{2,3},{3,2},{4,5},{5,4},{6,7},{7,6},{8,9},{9,8},{10,11... | collective-permute-start | bytes 3145736 | tf_op jit(solution)/shard_map/ppermute | solution.py:388
  16.8 113.9 %collective-permute-start.8 = (f32[2,256,512]{2,1,0:T(8,128)}, f32[2,256,512]{2,1,0:T(8,128)}, u32[]{:S(2)}, u32[]{:S(2)}) collective-permute-start(f32[2,256,512]{2,1,0:T(8,128)} %get-tuple-element.44), channel_id=1, source_target_pairs={{0,30},{2,28},{4,26},{6,24},{8,22},{10,20},{12,18},{14,16},{16,14}... | collective-permute-start | bytes 3145736 | tf_op jit(solution)/shard_map/ppermute | solution.py:380
  108.3 39.7 %collective-permute-start.3 = (f32[2,256,512]{2,1,0:T(8,128)}, f32[2,256,512]{2,1,0:T(8,128)}, u32[]{:S(2)}, u32[]{:S(2)}) collective-permute-start(f32[2,256,512]{2,1,0:T(8,128)} %collective-permute-done.2.refs_4_), channel_id=1, source_target_pairs={{0,1},{1,0},{2,3},{3,2},{4,5},{5,4},{6,7},{7,6},{8,9},{9,8},{10,11... | collective-permute-start | bytes 3145736 | tf_op jit(solution)/shard_map/ppermute | solution.py:388
  108.6 67.0 %collective-permute-start.6 = (f32[2,256,512]{2,1,0:T(8,128)}, f32[2,256,512]{2,1,0:T(8,128)}, u32[]{:S(2)}, u32[]{:S(2)}) collective-permute-start(f32[2,256,512]{2,1,0:T(8,128)} %get-tuple-element.41), channel_id=1, source_target_pairs={{0,30},{2,28},{4,26},{6,24},{8,22},{10,20},{12,18},{14,16},{16,14}... | collective-permute-start | bytes 3145736 | tf_op jit(solution)/shard_map/ppermute | solution.py:380
  130.8 47.6 %collective-permute-start.9 = (f32[2,256,512]{2,1,0:T(8,128)}, f32[2,256,512]{2,1,0:T(8,128)}, u32[]{:S(2)}, u32[]{:S(2)}) collective-permute-start(f32[2,256,512]{2,1,0:T(8,128)} %collective-permute-done.8.refs_6_), channel_id=1, source_target_pairs={{0,1},{1,0},{2,3},{3,2},{4,5},{5,4},{6,7},{7,6},{8,9},{9,8},{10,11... | collective-permute-start | bytes 3145736 | tf_op jit(solution)/shard_map/ppermute | solution.py:388
  148.0 42.4 %collective-permute-start.4 = (f32[1,256,512]{2,1,0:T(8,128)}, f32[1,256,512]{2,1,0:T(8,128)S(1)}, u32[]{:S(2)}, u32[]{:S(2)}) collective-permute-start(f32[1,256,512]{2,1,0:T(8,128)} %get-tuple-element.40), channel_id=1, source_target_pairs={{0,30},{2,28},{4,26},{6,24},{8,22},{10,20},{12,18},{14,16},{16,14}... | collective-permute-start | bytes 1572872 | tf_op jit(solution)/shard_map/ppermute | solution.py:380
  175.6 24.2 %collective-permute-start.10 = (f32[1,256,512]{2,1,0:T(8,128)}, f32[1,256,512]{2,1,0:T(8,128)}, u32[]{:S(2)}, u32[]{:S(2)}) collective-permute-start(f32[1,256,512]{2,1,0:T(8,128)} %get-tuple-element.52), channel_id=1, source_target_pairs={{0,30},{2,28},{4,26},{6,24},{8,22},{10,20},{12,18},{14,16},{16,14}... | collective-permute-start | bytes 1572872 | tf_op jit(solution)/shard_map/ppermute | solution.py:380
  178.1 25.5 %collective-permute-start.7 = (f32[2,256,512]{2,1,0:T(8,128)}, f32[2,256,512]{2,1,0:T(8,128)}, u32[]{:S(2)}, u32[]{:S(2)}) collective-permute-start(f32[2,256,512]{2,1,0:T(8,128)} %collective-permute-done.6.refs_4_), channel_id=1, source_target_pairs={{0,1},{1,0},{2,3},{3,2},{4,5},{5,4},{6,7},{7,6},{8,9},{9,8},{10,11... | collective-permute-start | bytes 3145736 | tf_op jit(solution)/shard_map/ppermute | solution.py:388
  190.4 22.4 %copy-start.1 = (f32[1,256,512]{2,1,0:T(8,128)}, f32[1,256,512]{2,1,0:T(8,128)S(1)}, u32[]{:S(2)}) copy-start(f32[1,256,512]{2,1,0:T(8,128)S(1)} %collective-permute-done.4.refs_5_) | copy-start | bytes 1572868
  190.4 30.6 %collective-permute-start.13 = (f32[512,512]{1,0:T(8,128)}, f32[512,512]{1,0:T(8,128)}, u32[]{:S(2)}, u32[]{:S(2)}) collective-permute-start(f32[512,512]{1,0:T(8,128)} %get-tuple-element.63), channel_id=1, source_target_pairs={{0,2},{2,4},{4,6},{6,8},{8,10},{10,12},{12,14},{16,18},{18,20},{20... | collective-permute-start | bytes 3145736 | tf_op jit(solution)/shard_map/ppermute | solution.py:395
  192.4 33.9 %collective-permute-start.12 = (f32[512,512]{1,0:T(8,128)}, f32[512,512]{1,0:T(8,128)}, u32[]{:S(2)}, u32[]{:S(2)}) collective-permute-start(f32[512,512]{1,0:T(8,128)} %get-tuple-element.60), channel_id=1, source_target_pairs={{2,0},{4,2},{6,4},{8,6},{10,8},{12,10},{14,12},{18,16},{20,18},{22... | collective-permute-start | bytes 3145736 | tf_op jit(solution)/shard_map/ppermute | solution.py:396
  199.9 14.8 %collective-permute-start.11 = (f32[1,256,512]{2,1,0:T(8,128)}, f32[1,256,512]{2,1,0:T(8,128)}, u32[]{:S(2)}, u32[]{:S(2)}) collective-permute-start(f32[1,256,512]{2,1,0:T(8,128)} %collective-permute-done.10.refs_4_), channel_id=1, source_target_pairs={{0,1},{1,0},{2,3},{3,2},{4,5},{5,4},{6,7},{7,6},{8,9},{9,8},{10,11... | collective-permute-start | bytes 1572872 | tf_op jit(solution)/shard_map/ppermute | solution.py:388
  199.9 26.3 %collective-permute-start.5 = (f32[1,256,512]{2,1,0:T(8,128)S(1)}, f32[1,256,512]{2,1,0:T(8,128)}, u32[]{:S(2)}, u32[]{:S(2)}) collective-permute-start(f32[1,256,512]{2,1,0:T(8,128)S(1)} %collective-permute-done.4.refs_5_), channel_id=1, source_target_pairs={{0,1},{1,0},{2,3},{3,2},{4,5},{5,4},{6,7},{7,6},{8,9},{9,8},{10,11... | collective-permute-start | bytes 1572872 | tf_op jit(solution)/shard_map/ppermute | solution.py:388
